TPU v7x, 32 devices: a whole 2x2x4 slice. The times are simulated.
32 devices in a mesh: box: 4 (over y, core), dir: 8 (over z, x).
Axes of the slice: x: 2, y: 2, z: 4, core: 2. Of those that a mesh axis runs over, the one named last changes fastest.
Arguments:
- currents: bfloat16 [256, 2, 256, 128], P(('box', 'dir')), may hold values from -6 to 6
- near_blocks: bfloat16 [256, 3, 2, 256, 256], P(('box', 'dir')), may hold values from -0.21875 to 0.21875
- near_mask: int32 [2, 256], replicated, may hold values 0 or 1
- aggregate: bfloat16 [2, 512, 256], replicated, may hold values from -0.375 to 0.375
- disaggregate: bfloat16 [2, 256, 512], replicated, may hold values from -0.25 to 0.25
- centers: float32 [3, 256], replicated, may hold values from 0 to 16
Outputs:
- fields: bfloat16 [256, 2, 256, 128], P(('box', 'dir'))
All inputs are finite; a program needn't handle non-finite values.
Results may differ from a plain program's by a relative error of at most 0.0054.
Values may be sent and summed in bfloat16 or wider, within the bound.
No kernel may reach another device: no remote copies, remote signals or barrier semaphores. Data moves between devices by JAX's collectives and lax.ppermute only.
A program may use at most 64 MiB of HBM per device.

v0:
```python
import math

import jax
import jax.numpy as jnp
from jax import lax
from jax.sharding import PartitionSpec as P

wave_number = 2.0
far_gain = 8.0
golden_turn = 2.399963229728653


def extended(block, sides, width):
    for axis, dim in sides:
        count = lax.axis_size(axis)
        forward = [(i, i + 1) for i in range(count - 1)]
        backward = [(target, source) for source, target in forward]
        low = lax.ppermute(
            lax.slice_in_dim(block, block.shape[dim] - width, None, axis=dim), axis, forward
        )
        high = lax.ppermute(lax.slice_in_dim(block, 0, width, axis=dim), axis, backward)
        block = jnp.concatenate([low, block, high], axis=dim)
    return block


def direction_cosines(count, first, many):
    order = (first + jnp.arange(many, dtype=jnp.int32)).astype(jnp.float32)
    height = 1.0 - (2.0 * order + 1.0) / count
    radial = jnp.sqrt(1.0 - height * height)
    azimuth = order * golden_turn
    return (radial * jnp.cos(azimuth), radial * jnp.sin(azimuth), height)


def phase_angles(points, first, many, count):
    dir_x, dir_y, dir_z = direction_cosines(count, first, many)
    return wave_number * (
        points[0][:, None] * dir_x[None, :]
        + points[1][:, None] * dir_y[None, :]
        + points[2][:, None] * dir_z[None, :]
    )


def far_matrix(centers, near_mask):
    total_boxes = centers.shape[1]
    squared = jnp.zeros((total_boxes, total_boxes), jnp.float32)
    for axis_number in range(3):
        spread = centers[axis_number][:, None] - centers[axis_number][None, :]
        squared = squared + spread * spread
    spacing = jnp.sqrt(1.0 + squared)
    kernel = jnp.cos(wave_number * spacing) / (1.0 + spacing) * (far_gain / math.sqrt(total_boxes))
    rows = jnp.arange(total_boxes, dtype=jnp.int32)[:, None]
    cols = jnp.arange(total_boxes, dtype=jnp.int32)[None, :]
    linked = (
        (cols == rows)
        | (cols == rows - 1) & (near_mask[0][:, None] == 1)
        | (cols == rows + 1) & (near_mask[1][:, None] == 1)
    )
    return jnp.where(linked, 0.0, kernel).astype(jnp.bfloat16)


def near_field(currents, near_blocks, own_mask):
    padded = extended(currents, ((("box", "dir"), 0),), 1)
    left_on = own_mask[0].astype(jnp.bfloat16)[:, None, None, None]
    right_on = own_mask[1].astype(jnp.bfloat16)[:, None, None, None]
    stacked = jnp.stack([currents, padded[:-2] * left_on, padded[2:] * right_on], 1)

    def product(left, right):
        return jnp.einsum("bjuv,bjva->bua", left, right, preferred_element_type=jnp.float32)

    block_re = near_blocks[:, :, 0]
    block_im = near_blocks[:, :, 1]
    near_re = product(block_re, stacked[:, :, 0]) - product(block_im, stacked[:, :, 1])
    near_im = product(block_re, stacked[:, :, 1]) + product(block_im, stacked[:, :, 0])
    return jnp.stack([near_re, near_im], 1)


def local(currents, near_blocks, near_mask, aggregate, disaggregate, centers):
    device_index = lax.axis_index(("box", "dir"))
    devices = lax.axis_size(("box", "dir"))
    box_count = currents.shape[0]
    total_boxes = centers.shape[1]
    dir_count = aggregate.shape[1]
    dir_share = dir_count // devices
    angle_count = currents.shape[3]
    own_centers = lax.dynamic_slice_in_dim(centers, device_index * box_count, box_count, 1)
    own_mask = lax.dynamic_slice_in_dim(near_mask, device_index * box_count, box_count, 1)
    near = near_field(currents, near_blocks, own_mask)

    def gather_in(matrix, vectors):
        return jnp.einsum("ku,bua->bka", matrix, vectors, preferred_element_type=jnp.float32)

    pat_re = gather_in(aggregate[0], currents[:, 0]) - gather_in(aggregate[1], currents[:, 1])
    pat_im = gather_in(aggregate[0], currents[:, 1]) + gather_in(aggregate[1], currents[:, 0])
    theta = phase_angles(own_centers, 0, dir_count, dir_count)
    cosine = jnp.cos(theta)[:, :, None]
    sine = jnp.sin(theta)[:, :, None]
    pattern = jnp.stack(
        [cosine * pat_re + sine * pat_im, cosine * pat_im - sine * pat_re], 2
    ).astype(jnp.bfloat16)
    arrived = lax.all_to_all(pattern[None], ("box", "dir"), split_axis=2, concat_axis=0, tiled=True)
    flat_pattern = arrived.reshape(total_boxes, dir_share * 2 * angle_count)
    translate = far_matrix(centers, near_mask)
    summed = jnp.dot(translate, flat_pattern, preferred_element_type=jnp.float32).reshape(
        total_boxes, dir_share, 2, angle_count
    )
    theta_all = phase_angles(centers, device_index * dir_share, dir_share, dir_count)
    cos_all = jnp.cos(theta_all)[:, :, None]
    sin_all = jnp.sin(theta_all)[:, :, None]
    sum_re = summed[:, :, 0]
    sum_im = summed[:, :, 1]
    received = jnp.stack(
        [cos_all * sum_re - sin_all * sum_im, cos_all * sum_im + sin_all * sum_re], 2
    ).astype(jnp.bfloat16)
    shaped_back = received.reshape(devices, box_count, dir_share, 2, angle_count)
    returned = lax.all_to_all(shaped_back, ("box", "dir"), split_axis=0, concat_axis=2, tiled=True)
    returned = returned.reshape(box_count, dir_count, 2, angle_count)

    def spread_out(matrix, vectors):
        return jnp.einsum("uk,bka->bua", matrix, vectors, preferred_element_type=jnp.float32)

    far_re = spread_out(disaggregate[0], returned[:, :, 0]) - spread_out(
        disaggregate[1], returned[:, :, 1]
    )
    far_im = spread_out(disaggregate[0], returned[:, :, 1]) + spread_out(
        disaggregate[1], returned[:, :, 0]
    )
    far = jnp.stack([far_re, far_im], 1)
    return (near + far).astype(jnp.bfloat16)


def solution(mesh):
    return jax.shard_map(
        local,
        mesh=mesh,
        in_specs=(
            P(("box", "dir"), None, None, None),
            P(("box", "dir"), None, None, None, None),
            P(),
            P(),
            P(),
            P(),
        ),
        out_specs=P(("box", "dir"), None, None, None),
        check_vma=False,
    )
```

profile of v0, /device:TPU:17, one launch (start us, length us, event | category | flops | bytes accessed | tf_op | source)
XLA Modules:
  0.0 152.9 jit_solution(14616655353102153419)
XLA Ops:
  0.1 1.5 %copy.35 = bf16[8,2,256,128]{2,3,0,1:T(8,128)(2,1)S(1)} copy(bf16[8,2,256,128]{3,2,1,0:T(8,128)(2,1)} %param.6) | data formatting | bytes 2097152 | tf_op args[0]
  1.6 1.8 %fusion.50 = f32[8,128,512]{2,1,0:T(8,128)} fusion(bf16[8,2,256,128]{2,3,0,1:T(8,128)(2,1)S(1)} %copy.35, bf16[2,512,256]{2,1,0:T(8,128)(2,1)S(1)} %copy-done), kind=kOutput, calls=%fused_computation.54 | convolution fusion | flops 268435456 | bytes 2883584 | tf_op jit(solution)/shard_map/ku,bua->bka/dot_general | solution.py:90
  4.2 2.2 %convolution_add_fusion = f32[8,128,512]{2,1,0:T(8,128)S(1)} fusion(f32[8,128,512]{2,1,0:T(8,128)} %fusion.50, bf16[8,2,256,128]{2,3,0,1:T(8,128)(2,1)S(1)} %copy.35, bf16[2,512,256]{2,1,0:T(8,128)(2,1)} %param.9), kind=kOutput, calls=%fused_computation.21 | convolution fusion | flops 268959744 | bytes 4980736 | tf_op jit(solution)/shard_map/ku,bua->bka/dot_general | solution.py:90
  6.6 0.8 fusion.39
  7.6 3.1 %copy.44 = bf16[1,8,512,2,128]{4,1,3,0,2:T(8,128)(2,1)} copy(bf16[1,8,512,2,128]{2,4,1,3,0:T(8,128)(2,1)S(1)} %pad_maximum_fusion.1) | data formatting | bytes 4194304 | tf_op jit(solution)/shard_map/stack | solution.py:97
  10.7 6.2 %all-to-all-start = ((bf16[1,8,512,2,128]{4,1,3,0,2:T(8,128)(2,1)}), bf16[1,8,512,2,128]{4,1,3,0,2:T(8,128)(2,1)S(1)}, u32[]{:S(2)}, u32[]{:S(2)}) async-start(bf16[1,8,512,2,128]{4,1,3,0,2:T(8,128)(2,1)} %copy.44), calls=%async_computation | async-start | bytes 4194304 | tf_op jit(solution)/shard_map/all_to_all | solution.py:100
  17.2 44.8 %all-to-all-done = bf16[1,8,512,2,128]{4,1,3,0,2:T(8,128)(2,1)S(1)} async-done(((bf16[1,8,512,2,128]{4,1,3,0,2:T(8,128)(2,1)}), bf16[1,8,512,2,128]{4,1,3,0,2:T(8,128)(2,1)S(1)}, u32[]{:S(2)}, u32[]{:S(2)}) %all-to-all-start) | async-done | bytes 2097184 | tf_op jit(solution)/shard_map/all_to_all | solution.py:100
  62.5 3.2 %copy.46 = bf16[32,1,8,16,2,128]{5,4,3,2,0,1:T(2,128)(2,1)S(1)} copy(bf16[32,1,8,16,2,128]{5,3,0,4,2,1:T(8,128)(2,1)S(1)} %bitcast.191) | data formatting | bytes 4194304 | tf_op jit(solution)/shard_map/all_to_all | solution.py:100
  65.7 2.8 %reshape.499 = bf16[256,4096]{1,0:T(8,128)(2,1)} reshape(bf16[32,1,8,16,2,128]{5,4,3,2,0,1:T(2,128)(2,1)S(1)} %copy.46) | data formatting | bytes 4194304 | tf_op jit(solution)/shard_map/reshape | solution.py:101
  68.6 3.3 %copy.47 = bf16[4096,256]{1,0:T(8,128)(2,1)S(1)} copy(bf16[4096,256]{0,1:T(8,128)(2,1)} %bitcast.192) | data formatting | bytes 4194304 | tf_op jit(solution)/shard_map/dot_general | solution.py:103
  71.8 1.8 %fusion.72 = f32[256,16,2,128]{3,0,2,1:T(8,128)S(1)} fusion(bf16[16,2,128,256]{3,2,1,0:T(8,128)(2,1)S(1)} %bitcast.193, f32[256]{0:T(256)S(1)} %bitcast.199, f32[256]{0:T(256)S(1)} %bitcast.197, f32[256]{0:T(256)S(1)} %bitcast.195, s32[256]{0:T(256)S(1)} %get-tuple-element.29, s32[256]{0:T(256)S(1)} %get-tuple-element.30, ...), kind=kOutput, calls=%fused_computation.80 | convolution fusion | flops 538312704 | bytes 6297088 | tf_op jit(solution)/shard_map/dot_general | solution.py:103
  73.6 1.4 fusion.41
  75.1 1.2 copy.48
  76.3 1.2 copy.49
  77.5 1.5 pad_maximum_fusion.2
  79.0 7.8 %all-to-all-start.1 = ((bf16[32,8,16,2,128]{4,2,3,1,0:T(8,128)(2,1)}), bf16[32,8,16,2,128]{4,2,3,1,0:T(8,128)(2,1)S(1)}, u32[]{:S(2)}, u32[]{:S(2)}) async-start(bf16[32,8,16,2,128]{4,2,3,1,0:T(8,128)(2,1)} %pad_maximum_fusion.2), calls=%async_computation.1 | async-start | bytes 4194304 | tf_op jit(solution)/shard_map/all_to_all | solution.py:115
  86.9 3.1 %collective-permute-start = (bf16[1,2,256,128]{2,3,0,1:T(8,128)(2,1)S(1)}, bf16[1,2,256,128]{2,3,0,1:T(8,128)(2,1)S(1)}, u32[]{:S(2)}, u32[]{:S(2)}) collective-permute-start(bf16[1,2,256,128]{2,3,0,1:T(8,128)(2,1)S(1)} %get-tuple-element.13), channel_id=1, source_target_pairs={{0,1},{1,2},{2,3},{3,4},{4,5},{5,6},{6,7},{7,8},{8,9},{9,10},{10,1... | collective-permute-start | bytes 393224 | tf_op jit(solution)/shard_map/ppermute | solution.py:18
  90.0 3.3 %collective-permute-start.1 = (bf16[1,2,256,128]{2,3,0,1:T(8,128)(2,1)S(1)}, bf16[1,2,256,128]{2,3,0,1:T(8,128)(2,1)S(1)}, u32[]{:S(2)}, u32[]{:S(2)}) collective-permute-start(bf16[1,2,256,128]{2,3,0,1:T(8,128)(2,1)S(1)} %get-tuple-element.14), channel_id=1, source_target_pairs={{1,0},{2,1},{3,2},{4,3},{5,4},{6,5},{7,6},{8,7},{9,8},{10,9},{11,1... | collective-permute-start | bytes 393224 | tf_op jit(solution)/shard_map/ppermute | solution.py:21
  93.4 44.3 %collective-permute-done = bf16[1,2,256,128]{2,3,0,1:T(8,128)(2,1)S(1)} collective-permute-done((bf16[1,2,256,128]{2,3,0,1:T(8,128)(2,1)S(1)}, bf16[1,2,256,128]{2,3,0,1:T(8,128)(2,1)S(1)}, u32[]{:S(2)}, u32[]{:S(2)}) %collective-permute-start) | collective-permute-done | bytes 131104 | tf_op jit(solution)/shard_map/ppermute | solution.py:18
  138.2 3.3 %fusion.13 = f32[8,128,256]{2,1,0:T(8,128)S(1)} fusion(bf16[8,3,2,256,256]{4,3,2,1,0:T(8,128)(2,1)} %param.7, bf16[8,3,2,256,128]{3,4,1,0,2:T(8,128)(2,1)S(1)} %pad_maximum_fusion), kind=kOutput, calls=%fused_computation.25 | convolution fusion | flops 402653184 | bytes 5767168 | tf_op jit(solution)/shard_map/bjuv,bjva->bua/dot_general | solution.py:68
  141.6 1.1 fusion.16
  142.7 2.1 %fusion.36 = f32[8,1,256,128]{2,3,0,1:T(8,128)} fusion(f32[8,128,256]{2,1,0:T(8,128)S(1)} %fusion.13, bf16[8,3,2,256,256]{4,3,2,1,0:T(8,128)(2,1)S(1)} %bitcast.201, bf16[8,3,2,256,128]{3,4,1,0,2:T(8,128)(2,1)S(1)} %pad_maximum_fusion), kind=kOutput, calls=%fused_computation.36 | convolution fusion | flops 402915328 | bytes 6815744 | tf_op jit(solution)/shard_map/bjuv,bjva->bua/dot_general | solution.py:68
  144.8 2.1 %fusion.30 = f32[8,1,256,128]{2,3,0,1:T(8,128)} fusion(f32[8,128,256]{2,1,0:T(8,128)S(1)} %fusion.16, bf16[8,3,2,256,256]{4,3,2,1,0:T(8,128)(2,1)S(1)} %bitcast.201, bf16[8,3,2,256,128]{3,4,1,0,2:T(8,128)(2,1)S(1)} %pad_maximum_fusion), kind=kOutput, calls=%fused_computation.34 | convolution fusion | flops 402915328 | bytes 6815744 | tf_op jit(solution)/shard_map/bjuv,bjva->bua/dot_general | solution.py:68
  151.6 1.3 copy.53
  (50 shorter events, 7.2 us)
Async XLA Ops:
  0.0 1.6 %copy-start = (bf16[2,512,256]{2,1,0:T(8,128)(2,1)S(1)}, bf16[2,512,256]{2,1,0:T(8,128)(2,1)}, u32[]{:S(2)}) copy-start(bf16[2,512,256]{2,1,0:T(8,128)(2,1)} %param.9) | copy-start | bytes 1572868
  1.6 1.8 %copy-start.1 = (bf16[2,512,256]{2,1,0:T(8,128)(2,1)S(1)}, bf16[2,512,256]{2,1,0:T(8,128)(2,1)}, u32[]{:S(2)}) copy-start(bf16[2,512,256]{2,1,0:T(8,128)(2,1)} %param.9) | copy-start | bytes 1572868
  3.4 0.7 copy-start.7
  4.2 2.4 %copy-start.2 = (bf16[2,512,256]{2,1,0:T(8,128)(2,1)S(1)}, bf16[2,512,256]{2,1,0:T(8,128)(2,1)}, u32[]{:S(2)}) copy-start(bf16[2,512,256]{2,1,0:T(8,128)(2,1)} %param.9) | copy-start | bytes 1572868
  10.7 6.3 %copy-start.8 = (s32[2,256]{1,0:T(2,128)S(1)}, s32[2,256]{1,0:T(2,128)}, u32[]{:S(2)}) copy-start(s32[2,256]{1,0:T(2,128)} %param.8) | copy-start | bytes 6148
  10.7 51.3 %all-to-all-start = ((bf16[1,8,512,2,128]{4,1,3,0,2:T(8,128)(2,1)}), bf16[1,8,512,2,128]{4,1,3,0,2:T(8,128)(2,1)S(1)}, u32[]{:S(2)}, u32[]{:S(2)}) async-start(bf16[1,8,512,2,128]{4,1,3,0,2:T(8,128)(2,1)} %copy.44), calls=%async_computation | async-start | bytes 4194304 | tf_op jit(solution)/shard_map/all_to_all | solution.py:100
  79.0 68.0 %all-to-all-start.1 = ((bf16[32,8,16,2,128]{4,2,3,1,0:T(8,128)(2,1)}), bf16[32,8,16,2,128]{4,2,3,1,0:T(8,128)(2,1)S(1)}, u32[]{:S(2)}, u32[]{:S(2)}) async-start(bf16[32,8,16,2,128]{4,2,3,1,0:T(8,128)(2,1)} %pad_maximum_fusion.2), calls=%async_computation.1 | async-start | bytes 4194304 | tf_op jit(solution)/shard_map/all_to_all | solution.py:115
  86.9 50.8 %collective-permute-start = (bf16[1,2,256,128]{2,3,0,1:T(8,128)(2,1)S(1)}, bf16[1,2,256,128]{2,3,0,1:T(8,128)(2,1)S(1)}, u32[]{:S(2)}, u32[]{:S(2)}) collective-permute-start(bf16[1,2,256,128]{2,3,0,1:T(8,128)(2,1)S(1)} %get-tuple-element.13), channel_id=1, source_target_pairs={{0,1},{1,2},{2,3},{3,4},{4,5},{5,6},{6,7},{7,8},{8,9},{9,10},{10,1... | collective-permute-start | bytes 393224 | tf_op jit(solution)/shard_map/ppermute | solution.py:18
  90.0 47.7 %collective-permute-start.1 = (bf16[1,2,256,128]{2,3,0,1:T(8,128)(2,1)S(1)}, bf16[1,2,256,128]{2,3,0,1:T(8,128)(2,1)S(1)}, u32[]{:S(2)}, u32[]{:S(2)}) collective-permute-start(bf16[1,2,256,128]{2,3,0,1:T(8,128)(2,1)S(1)} %get-tuple-element.14), channel_id=1, source_target_pairs={{1,0},{2,1},{3,2},{4,3},{5,4},{6,5},{7,6},{8,7},{9,8},{10,9},{11,1... | collective-permute-start | bytes 393224 | tf_op jit(solution)/shard_map/ppermute | solution.py:21
  137.7 3.9 %slice-start = ((s8[6291456]{0:T(1024)(128)(4,1)}), s8[4194304]{0:T(1024)(128)(4,1)S(1)}, s32[]{:S(2)}) async-start(s8[6291456]{0:T(1024)(128)(4,1)} %bitcast.200), calls=%async_computation.2 | async-start | bytes 8388608
  137.9 3.7 %slice-start.1 = ((s8[6291456]{0:T(1024)(128)(4,1)}), s8[2097152]{0:T(1024)(128)(4,1)S(1)}, s32[]{:S(2)}) async-start(s8[6291456]{0:T(1024)(128)(4,1)} %bitcast.200), calls=%async_computation.3 | async-start | bytes 4194304
  147.0 1.0 copy-start.3
  148.0 1.0 copy-start.4
  149.5 1.2 copy-start.5
  149.6 1.5 %copy-start.6 = (f32[8,1,256,128]{2,3,0,1:T(8,128)S(1)}, f32[8,1,256,128]{2,3,0,1:T(8,128)}, u32[]{:S(2)}) copy-start(f32[8,1,256,128]{2,3,0,1:T(8,128)} %fusion.30) | copy-start | bytes 3145732
where the time goes:
time: 153 us
  waiting for transfers between devices  89.1 us (58%)
  local copies, waits for them, and re-layouts  20.7 us (14%)
  starting transfers between devices  20.5 us (13%)
  matrix products  17.7 us (12%)
  other arithmetic  4.68 us (3%)
    all_to_all x1, waiting for transfers between devices, local(): lax.all_to_all(pattern[None], ('box', 'dir'), split_axis=2, concat_axis=0...  44.8 us
    ppermute x1, waiting for transfers between devices, extended(): lax.ppermute(lax.slice_in_dim(block, block.shape[dim] - width, None, axis...  44.3 us
    dot_general x4, matrix products, product(): jnp.einsum('bjuv,bjva->bua', left, right, preferred_element_type=jnp.floa...  8.69 us
    all_to_all x1, starting transfers between devices, local(): lax.all_to_all(shaped_back, ('box', 'dir'), split_axis=0, concat_axis=2,...  7.83 us
    all_to_all x1, starting transfers between devices, local(): lax.all_to_all(pattern[None], ('box', 'dir'), split_axis=2, concat_axis=0...  6.23 us
    dot_general x4, matrix products, gather_in(): jnp.einsum('ku,bua->bka', matrix, vectors, preferred_element_type=jnp.flo...  5.26 us
    all_to_all x2, local copies, waits for them, and re-layouts, local(): lax.all_to_all(pattern[None], ('box', 'dir'), split_axis=2, concat_axis=0...  3.78 us
    unnamed x23, local copies, waits for them, and re-layouts  3.38 us
  transfers between devices with their start and end apart: 4, of which 2 were waited for; matrix products, arithmetic and copies ran while one was open for 6% of the time, Pallas kernels for 0%

commit v1 on v0

v1 whole, which is shorter than its diff:
```python
import functools
import math

import jax
import jax.numpy as jnp
from jax import lax
from jax.experimental import pallas as pl
from jax.experimental.pallas import tpu as pltpu
from jax.sharding import PartitionSpec as P

wave_number = 2.0
far_gain = 8.0
golden_turn = 2.399963229728653
axes = ("box", "dir")
chunks_wanted = 1


def direction_cosines(count):
    order = jnp.arange(count, dtype=jnp.int32).astype(jnp.float32)
    height = 1.0 - (2.0 * order + 1.0) / count
    radial = jnp.sqrt(1.0 - height * height)
    azimuth = order * golden_turn
    return (radial * jnp.cos(azimuth), radial * jnp.sin(azimuth), height)


def phase_angles(points, count):
    dir_x, dir_y, dir_z = direction_cosines(count)
    return wave_number * (
        points[0][:, None] * dir_x[None, :]
        + points[1][:, None] * dir_y[None, :]
        + points[2][:, None] * dir_z[None, :]
    )


def far_matrix(centers, near_mask):
    total_boxes = centers.shape[1]
    squared = jnp.zeros((total_boxes, total_boxes), jnp.float32)
    for axis_number in range(3):
        spread = centers[axis_number][:, None] - centers[axis_number][None, :]
        squared = squared + spread * spread
    spacing = jnp.sqrt(1.0 + squared)
    kernel = jnp.cos(wave_number * spacing) / (1.0 + spacing) * (far_gain / math.sqrt(total_boxes))
    rows = jnp.arange(total_boxes, dtype=jnp.int32)[:, None]
    cols = jnp.arange(total_boxes, dtype=jnp.int32)[None, :]
    linked = (
        (cols == rows)
        | (cols == rows - 1) & (near_mask[0][:, None] == 1)
        | (cols == rows + 1) & (near_mask[1][:, None] == 1)
    )
    return jnp.where(linked, 0.0, kernel).astype(jnp.bfloat16)


def swap_matrix(outer, inner):
    size = outer * inner
    row = lax.broadcasted_iota(jnp.int32, (size, size), 0)
    col = lax.broadcasted_iota(jnp.int32, (size, size), 1)
    return ((row % inner) * outer + row // inner == col).astype(jnp.bfloat16)


def pack_body(currents_ref, swap_ref, *refs, devices, angles_each, group):
    outs, turned_ref = refs[:-1], refs[-1]
    boxes, _, unknowns, angles = currents_ref.shape
    rows = 2 * boxes
    for part in range(2):
        for box in range(boxes):
            turned_ref[part * boxes + box] = currents_ref[box, part].T
    per_out = angles_each // len(outs)
    for first in range(0, angles, group):
        own, device = divmod(first, devices)
        tile = turned_ref[:, first : first + group, :].reshape(rows * group, unknowns)
        mixed = jnp.dot(swap_ref[...], tile, preferred_element_type=jnp.float32)
        which, slot = divmod(own, per_out)
        outs[which][device : device + group, slot] = mixed.astype(jnp.bfloat16).reshape(
            group, rows, unknowns
        )


def pack(currents, devices, chunks):
    boxes, _, unknowns, angles = currents.shape
    angles_each = angles // devices
    group = math.gcd(16, devices)
    rows = 2 * boxes
    body = functools.partial(pack_body, devices=devices, angles_each=angles_each, group=group)
    shape = jax.ShapeDtypeStruct((devices, angles_each // chunks, rows, unknowns), jnp.bfloat16)
    return pl.pallas_call(
        body,
        out_shape=[shape] * chunks,
        scratch_shapes=[pltpu.VMEM((rows, angles, unknowns), jnp.bfloat16)],
        name="pack",
    )(currents, swap_matrix(group, rows))


def unpack_body(near_ref, swap_ref, *refs, devices, angles_each, group):
    ins, out_ref, turned_ref = refs[:-2], refs[-2], refs[-1]
    boxes, _, unknowns, angles = out_ref.shape
    rows = 2 * boxes
    per_in = angles_each // len(ins)
    for first in range(0, angles, group):
        own, device = divmod(first, devices)
        which, slot = divmod(own, per_in)
        tile = ins[which][device : device + group, slot].reshape(rows * group, unknowns)
        mixed = jnp.dot(swap_ref[...], tile, preferred_element_type=jnp.float32)
        turned_ref[:, first : first + group, :] = mixed.astype(jnp.bfloat16).reshape(
            rows, group, unknowns
        )
    for part in range(2):
        for box in range(boxes):
            far = turned_ref[part * boxes + box].T.astype(jnp.float32)
            out_ref[box, part] = (near_ref[box, part] + far).astype(jnp.bfloat16)


def unpack(near, pieces, devices):
    boxes, _, unknowns, angles = near.shape
    angles_each = angles // devices
    group = math.gcd(16, devices)
    rows = 2 * boxes
    body = functools.partial(unpack_body, devices=devices, angles_each=angles_each, group=group)
    return pl.pallas_call(
        body,
        out_shape=jax.ShapeDtypeStruct(near.shape, jnp.bfloat16),
        scratch_shapes=[pltpu.VMEM((rows, angles, unknowns), jnp.bfloat16)],
        name="unpack",
    )(near, swap_matrix(rows, group), *pieces)


def far_body(arrived_ref, gather_ref, spread_ref, translate_ref, cos_ref, sin_ref, out_ref, sum_ref):
    devices, _, rows, unknowns = arrived_ref.shape
    boxes = rows // 2
    total = devices * boxes
    width = cos_ref.shape[1]
    block = pl.program_id(1)
    arrived = arrived_ref[:, 0].reshape(devices * rows, unknowns)
    by_re = jnp.dot(arrived, gather_ref[0], preferred_element_type=jnp.float32)
    by_im = jnp.dot(arrived, gather_ref[1], preferred_element_type=jnp.float32)
    by_re = by_re.reshape(devices, 2, boxes, width)
    by_im = by_im.reshape(devices, 2, boxes, width)
    pat_re = (by_re[:, 0] - by_im[:, 1]).reshape(total, width)
    pat_im = (by_re[:, 1] + by_im[:, 0]).reshape(total, width)
    cosine = cos_ref[...]
    sine = sin_ref[...]
    out_re = (cosine * pat_re + sine * pat_im).astype(jnp.bfloat16)
    out_im = (cosine * pat_im - sine * pat_re).astype(jnp.bfloat16)
    translate = translate_ref[...]
    sum_re = jnp.dot(translate, out_re, preferred_element_type=jnp.float32)
    sum_im = jnp.dot(translate, out_im, preferred_element_type=jnp.float32)
    rec_re = (cosine * sum_re - sine * sum_im).astype(jnp.bfloat16)
    rec_im = (cosine * sum_im + sine * sum_re).astype(jnp.bfloat16)
    far = jnp.dot(rec_re, spread_ref[0], preferred_element_type=jnp.float32) + jnp.dot(
        rec_im, spread_ref[1], preferred_element_type=jnp.float32
    )

    @pl.when(block == 0)
    def _():
        sum_ref[...] = far

    @pl.when(block != 0)
    def _():
        sum_ref[...] += far

    @pl.when(block == pl.num_programs(1) - 1)
    def _():
        whole = sum_ref[...]
        real = whole[:, :unknowns].reshape(devices, 1, boxes, unknowns)
        imag = whole[:, unknowns:].reshape(devices, 1, boxes, unknowns)
        both = jnp.concatenate([real, imag], 1).reshape(devices, rows, unknowns)
        out_ref[:, 0] = both.astype(jnp.bfloat16)


def far_field(arrived, gather, spread, translate, cosine, sine):
    devices, slots, rows, unknowns = arrived.shape
    total, count = cosine.shape
    width = math.gcd(count, 256)
    return pl.pallas_call(
        far_body,
        grid=(slots, count // width),
        in_specs=[
            pl.BlockSpec((devices, 1, rows, unknowns), lambda i, j: (0, i, 0, 0)),
            pl.BlockSpec((2, unknowns, width), lambda i, j: (0, 0, j)),
            pl.BlockSpec((2, width, 2 * unknowns), lambda i, j: (0, j, 0)),
            pl.BlockSpec((total, total), lambda i, j: (0, 0)),
            pl.BlockSpec((total, width), lambda i, j: (0, j)),
            pl.BlockSpec((total, width), lambda i, j: (0, j)),
        ],
        out_specs=pl.BlockSpec((devices, 1, rows, unknowns), lambda i, j: (0, i, 0, 0)),
        out_shape=jax.ShapeDtypeStruct(arrived.shape, jnp.bfloat16),
        scratch_shapes=[pltpu.VMEM((total, 2 * unknowns), jnp.float32)],
        name="far",
    )(arrived, gather, spread, translate, cosine, sine)


def near_body(place_ref, mask_ref, currents_ref, low_ref, high_ref, blocks_ref, out_ref):
    boxes, _, unknowns, angles = currents_ref.shape
    box = pl.program_id(0)
    own = place_ref[0] * boxes + box

    def both(block):
        return jnp.concatenate([block[0], block[1]], 1)

    zero = jnp.zeros((unknowns, 2 * angles), jnp.bfloat16)
    here = both(currents_ref[box])
    before = jnp.where(box == 0, both(low_ref[0]), both(currents_ref[jnp.maximum(box - 1, 0)]))
    after = jnp.where(
        box == boxes - 1, both(high_ref[0]), both(currents_ref[jnp.minimum(box + 1, boxes - 1)])
    )
    before = jnp.where(mask_ref[0, own] == 1, before, zero)
    after = jnp.where(mask_ref[1, own] == 1, after, zero)
    by_re = jnp.zeros((unknowns, 2 * angles), jnp.float32)
    by_im = jnp.zeros((unknowns, 2 * angles), jnp.float32)
    for which, vectors in enumerate((here, before, after)):
        by_re += jnp.dot(blocks_ref[0, which, 0], vectors, preferred_element_type=jnp.float32)
        by_im += jnp.dot(blocks_ref[0, which, 1], vectors, preferred_element_type=jnp.float32)
    out_ref[0, 0] = by_re[:, :angles] - by_im[:, angles:]
    out_ref[0, 1] = by_re[:, angles:] + by_im[:, :angles]


def near_field(currents, low, high, near_blocks, near_mask, place):
    boxes, _, unknowns, angles = currents.shape
    whole = pl.BlockSpec(currents.shape, lambda i, *_: (0, 0, 0, 0))
    edge = pl.BlockSpec(low.shape, lambda i, *_: (0, 0, 0, 0))
    return pl.pallas_call(
        near_body,
        grid_spec=pltpu.PrefetchScalarGridSpec(
            num_scalar_prefetch=2,
            grid=(boxes,),
            in_specs=[
                whole,
                edge,
                edge,
                pl.BlockSpec((1, 3, 2, unknowns, unknowns), lambda i, *_: (i, 0, 0, 0, 0)),
            ],
            out_specs=pl.BlockSpec((1, 2, unknowns, angles), lambda i, *_: (i, 0, 0, 0)),
        ),
        out_shape=jax.ShapeDtypeStruct(currents.shape, jnp.float32),
        name="near",
    )(place, near_mask, currents, low, high, near_blocks)


def edges(currents):
    count = lax.axis_size(axes)
    forward = [(i, i + 1) for i in range(count - 1)]
    backward = [(i + 1, i) for i in range(count - 1)]
    low = lax.ppermute(currents[-1:], axes, forward)
    high = lax.ppermute(currents[:1], axes, backward)
    return low, high


def local(currents, near_blocks, near_mask, aggregate, disaggregate, centers):
    devices = lax.axis_size(axes)
    angles_each = currents.shape[3] // devices
    chunks = math.gcd(chunks_wanted, angles_each)
    dir_count = aggregate.shape[1]
    place = lax.axis_index(axes).astype(jnp.int32).reshape(1)

    packed = pack(currents, devices, chunks)
    arrived = [lax.all_to_all(x, axes, split_axis=0, concat_axis=0, tiled=True) for x in packed]
    low, high = edges(currents)
    gather = aggregate.transpose(0, 2, 1)
    turned = disaggregate.transpose(0, 2, 1)
    spread = jnp.stack(
        [
            jnp.concatenate([turned[0], turned[1]], 1),
            jnp.concatenate([-turned[1], turned[0]], 1),
        ]
    )
    translate = far_matrix(centers, near_mask)
    theta = phase_angles(centers, dir_count)
    cosine = jnp.cos(theta)
    sine = jnp.sin(theta)
    far = [far_field(x, gather, spread, translate, cosine, sine) for x in arrived]
    pieces = [lax.all_to_all(x, axes, split_axis=0, concat_axis=0, tiled=True) for x in far]
    near = near_field(currents, low, high, near_blocks, near_mask, place)
    return unpack(near, pieces, devices)


def solution(mesh):
    return jax.shard_map(
        local,
        mesh=mesh,
        in_specs=(
            P(axes, None, None, None),
            P(axes, None, None, None, None),
            P(),
            P(),
            P(),
            P(),
        ),
        out_specs=P(axes, None, None, None),
        check_vma=False,
    )
```

time: 153 us -> 94.3 us (0.62)
  waiting for transfers between devices: 89.1 us -> 34 us
  Pallas kernels: 0 us -> 25.9 us
  matrix products: 17.7 us -> 0 us
  local copies, waits for them, and re-layouts: 20.7 us -> 6.99 us
  other arithmetic: 4.68 us -> 7.45 us
    all_to_all x2, waiting for transfers between devices: 44.8 us -> 13.6 us  [local(): lax.all_to_all(x, axes, split_axis=0, concat_axis=0, tiled=True)]
    pallas_call x0 -> x4, Pallas kernels: none -> 25.9 us  [the longest x1 10.4 us: far_field(): pl.pallas_call(far_body, grid=(slots, count // width), in_specs=[pl.Block...]
    ppermute x2, waiting for transfers between devices: 44.3 us -> 20.4 us  [the longest x1 20.4 us: edges(): low = lax.ppermute(currents[-1:], axes, forward)]
    dot_general x13 -> x0, matrix products: 17.7 us -> none  [the longest x4 8.69 us: product(): jnp.einsum('bjuv,bjva->bua', left, right, preferred_element_type=jnp.floa...]
    another operation x3 -> x0, local copies, waits for them, and re-layouts: 5.51 us -> none  [the longest x1 3.07 us: local(): jnp.stack([cosine * pat_re + sine * pat_im, cosine * pat_im - sine * pat_...]
    all_to_all x3 -> x0, local copies, waits for them, and re-layouts: 4.32 us -> none  [the longest x2 3.78 us: local(): lax.all_to_all(pattern[None], ('box', 'dir'), split_axis=2, concat_axis=0...]
    dot_general x1 -> x0, local copies, waits for them, and re-layouts: 3.27 us -> none  [local(): jnp.dot(translate, flat_pattern, preferred_element_type=jnp.float32)]
    sin x0 -> x1, other arithmetic: none -> 3.18 us  [local(): sine = jnp.sin(theta)]
  transfers between devices with their start and end apart: 4 -> 4, of which waited for: 2 -> 2; matrix products, arithmetic and copies ran while one was open for 6% -> 12% of each run, Pallas kernels for 0% -> 10%
where the time goes in v1:
time: 94.3 us; the launch traced here: 93.4 us
  waiting for transfers between devices  34 us (36%)
  Pallas kernels  25.9 us (27%)
  starting transfers between devices  19 us (20%)
  other arithmetic  7.45 us (8%)
  local copies, waits for them, and re-layouts  6.99 us (7%)
    ppermute x1, waiting for transfers between devices, edges(): low = lax.ppermute(currents[-1:], axes, forward)  20.4 us
    all_to_all x2, waiting for transfers between devices, local(): lax.all_to_all(x, axes, split_axis=0, concat_axis=0, tiled=True)  13.6 us
    all_to_all x2, starting transfers between devices, local(): lax.all_to_all(x, axes, split_axis=0, concat_axis=0, tiled=True)  12.8 us
    pallas_call x1, Pallas kernels, far_field(): pl.pallas_call(far_body, grid=(slots, count // width), in_specs=[pl.Block...  10.4 us
    pallas_call x1, Pallas kernels, near_field(): pl.pallas_call(near_body, grid_spec=pltpu.PrefetchScalarGridSpec(num_scal...  8.96 us
    unnamed x14, local copies, waits for them, and re-layouts  5.96 us
    pallas_call x1, Pallas kernels, unpack(): pl.pallas_call(body, out_shape=jax.ShapeDtypeStruct(near.shape, jnp.bfloa...  3.6 us
    sin x1, other arithmetic, local(): sine = jnp.sin(theta)  3.18 us
  transfers between devices with their start and end apart: 4, of which 2 were waited for; matrix products, arithmetic and copies ran while one was open for 12% of the time, Pallas kernels for 10%

profile of v1, /device:TPU:17, one launch (start us, length us, event | category | flops | bytes accessed | tf_op | source)
XLA Modules:
  0.0 93.4 jit_solution(8570840452920721578)
XLA Ops:
  0.0 0.9 fusion.2.swap_ref
  1.0 2.9 %pack.1 = bf16[32,4,16,256]{3,2,1,0:T(8,128)(2,1)} custom-call(bf16[8,2,256,128]{3,2,1,0:T(8,128)(2,1)} %currents_ref.3, bf16[256,256]{1,0:T(8,128)(2,1)} %fusion.2.swap_ref), custom_call_target="tpu_custom_call" | custom-call | tf_op jit(solution)/shard_map/pack/pallas_call | solution.py:85
  3.9 6.2 %all-to-all-start = ((bf16[32,4,16,256]{3,2,1,0:T(8,128)(2,1)}), bf16[32,4,16,256]{3,2,1,0:T(8,128)(2,1)S(1)}, u32[]{:S(2)}, u32[]{:S(2)}) async-start(bf16[32,4,16,256]{3,2,1,0:T(8,128)(2,1)} %pack.1), calls=%async_computation | async-start | bytes 2097152 | tf_op jit(solution)/shard_map/all_to_all | solution.py:255
  10.1 1.2 %copy.8 = bf16[2,256,512]{1,2,0:T(8,128)(2,1)S(1)} copy(bf16[2,256,512]{2,1,0:T(8,128)(2,1)} %param.10) | data formatting | bytes 1048576 | tf_op args[4]
  11.3 2.1 %copy.7 = bf16[2,512,256]{1,2,0:T(8,128)(2,1)} copy(bf16[2,512,256]{2,1,0:T(8,128)(2,1)} %param.9) | data formatting | bytes 1048576 | tf_op args[3]
  13.6 0.1 maximum_bitcast_fusion
  13.7 1.1 %pad_maximum_fusion.spread_ref = bf16[2,512,512]{2,1,0:T(8,128)(2,1)} fusion(bf16[1,512,512]{2,1,0:T(8,128)(2,1)S(1)} %get-tuple-element.12, bf16[1,512,512]{2,1,0:T(8,128)(2,1)S(1)} %get-tuple-element.11), kind=kLoop, calls=%fused_computation | loop fusion | flops 524288 | bytes 2097152 | tf_op jit(solution)/shard_map/stack | solution.py:259
  14.7 2.1 %select_convert_fusion.translate_ref = bf16[256,256]{1,0:T(8,128)(2,1)} fusion(f32[256]{0:T(256)S(1)} %bitcast.21, f32[256]{0:T(256)S(1)} %bitcast.23, f32[256]{0:T(256)S(1)} %bitcast.19, s32[256]{0:T(256)S(1)} %get-tuple-element.24, s32[256]{0:T(256)S(1)} %get-tuple-element.25, pred[256]{0:T(512)(128)(4,1)S(1)} %get-tuple-element.6, ...), kind=kLoop, calls=%fused_computation.8 | loop fusion | flops 1441792 | bytes 136704 | tf_op jit(solution)/shard_map/convert_element_type | solution.py:50
  16.8 3.2 %fusion = (f32[256,512]{1,0:T(8,128)}, f32[256,512]{1,0:T(8,128)}) fusion(f32[512]{0:T(512)S(1)} %multiply_subtract_fusion, f32[256]{0:T(256)S(1)} %bitcast.22, f32[512]{0:T(512)S(1)} %get-tuple-element.26, f32[256]{0:T(256)S(1)} %bitcast.24, f32[512]{0:T(512)S(1)} %get-tuple-element.27, f32[256]{0:T(256)S(1)} %bitcast.20), kind=kLoop, calls=%fused_computation.4 | loop fusion | flops 786432 | bytes 1057792 | tf_op jit(solution)/shard_map/sin | solution.py:268
  20.0 13.6 %all-to-all-done.arrived_ref = bf16[32,4,16,256]{3,2,1,0:T(8,128)(2,1)S(1)} async-done(((bf16[32,4,16,256]{3,2,1,0:T(8,128)(2,1)}), bf16[32,4,16,256]{3,2,1,0:T(8,128)(2,1)S(1)}, u32[]{:S(2)}, u32[]{:S(2)}) %all-to-all-start) | async-done | bytes 1048608 | tf_op jit(solution)/shard_map/all_to_all | solution.py:255
  33.6 1.0 %copy-done = bf16[32,4,16,256]{3,2,1,0:T(8,128)(2,1)} copy-done((bf16[32,4,16,256]{3,2,1,0:T(8,128)(2,1)}, bf16[32,4,16,256]{3,2,1,0:T(8,128)(2,1)S(1)}, u32[]{:S(2)}) %copy-start) | copy-done | bytes 1048600
  34.6 10.4 %far.1 = bf16[32,4,16,256]{3,2,1,0:T(8,128)(2,1)} custom-call(bf16[32,4,16,256]{3,2,1,0:T(8,128)(2,1)} %copy-done, bf16[2,256,512]{2,1,0:T(8,128)(2,1)} %bitcast.18, bf16[2,512,512]{2,1,0:T(8,128)(2,1)} %pad_maximum_fusion.spread_ref, bf16[256,256]{1,0:T(8,128)(2,1)} %select_convert_fusion.translate_ref, f32[256,512]{1,0:T(8,128)} %get-tuple-element.14.cos_ref, ...), custom_call_target="tpu_custom_call" | custom-call | tf_op jit(solution)/shard_map/far/pallas_call | solution.py:173
  45.0 6.6 %all-to-all-start.1 = ((bf16[32,4,16,256]{3,2,1,0:T(8,128)(2,1)}), bf16[32,4,16,256]{3,2,1,0:T(8,128)(2,1)S(1)}, u32[]{:S(2)}, u32[]{:S(2)}) async-start(bf16[32,4,16,256]{3,2,1,0:T(8,128)(2,1)} %far.1), calls=%async_computation.1 | async-start | bytes 2097152 | tf_op jit(solution)/shard_map/all_to_all | solution.py:270
  51.6 1.0 %fusion.10 = (bf16[1,2,256,128]{3,2,1,0:T(8,128)(2,1)S(1)}, bf16[1,2,256,128]{3,2,1,0:T(8,128)(2,1)S(1)}) fusion(bf16[8,2,256,128]{3,2,1,0:T(8,128)(2,1)} %currents_ref.3), kind=kLoop, calls=%fused_computation.36 | loop fusion | bytes 524288 | tf_op jit(solution)/shard_map/slice | solution.py:243
  52.6 3.1 %collective-permute-start = (bf16[1,2,256,128]{3,2,1,0:T(8,128)(2,1)S(1)}, bf16[1,2,256,128]{3,2,1,0:T(8,128)(2,1)S(1)}, u32[]{:S(2)}, u32[]{:S(2)}) collective-permute-start(bf16[1,2,256,128]{3,2,1,0:T(8,128)(2,1)S(1)} %get-tuple-element.8), channel_id=1, source_target_pairs={{0,1},{1,2},{2,3},{3,4},{4,5},{5,6},{6,7},{7,8},{8,9},{9,10},{10,1... | collective-permute-start | bytes 393224 | tf_op jit(solution)/shard_map/ppermute | solution.py:242
  55.7 3.1 %collective-permute-start.1 = (bf16[1,2,256,128]{3,2,1,0:T(8,128)(2,1)S(1)}, bf16[1,2,256,128]{3,2,1,0:T(8,128)(2,1)S(1)}, u32[]{:S(2)}, u32[]{:S(2)}) collective-permute-start(bf16[1,2,256,128]{3,2,1,0:T(8,128)(2,1)S(1)} %get-tuple-element.7), channel_id=1, source_target_pairs={{1,0},{2,1},{3,2},{4,3},{5,4},{6,5},{7,6},{8,7},{9,8},{10,9},{11,1... | collective-permute-start | bytes 393224 | tf_op jit(solution)/shard_map/ppermute | solution.py:243
  58.8 20.4 %collective-permute-done.low_ref = bf16[1,2,256,128]{3,2,1,0:T(8,128)(2,1)S(1)} collective-permute-done((bf16[1,2,256,128]{3,2,1,0:T(8,128)(2,1)S(1)}, bf16[1,2,256,128]{3,2,1,0:T(8,128)(2,1)S(1)}, u32[]{:S(2)}, u32[]{:S(2)}) %collective-permute-start) | collective-permute-done | bytes 131104 | tf_op jit(solution)/shard_map/ppermute | solution.py:242
  79.2 0.0 collective-permute-done.1.high_ref
  79.2 0.6 copy-done.2
  79.9 0.1 copy-done.3
  79.9 9.0 %near.1.near_ref = f32[8,2,256,128]{3,2,1,0:T(8,128)} custom-call(s32[1]{0:T(128)} %bitcast.place_ref, s32[2,256]{1,0:T(2,128)} %mask_ref.1, bf16[8,2,256,128]{3,2,1,0:T(8,128)(2,1)} %currents_ref.3, bf16[1,2,256,128]{3,2,1,0:T(8,128)(2,1)} %copy-done.2, bf16[1,2,256,128]{3,2,1,0:T(8,128)(2,1)} %copy-done.3, bf16[8,3,2,256,256]{4,3,2,1,0:T(8,128)(2,1)} %blocks_ref.1), custom_call_target="tpu_custom_call" | custom-call | tf_op jit(solution)/shard_map/near/pallas_call | solution.py:220
  88.9 0.0 all-to-all-done.1.refs_0_
  88.9 1.0 %copy-done.1 = bf16[32,4,16,256]{3,2,1,0:T(8,128)(2,1)} copy-done((bf16[32,4,16,256]{3,2,1,0:T(8,128)(2,1)}, bf16[32,4,16,256]{3,2,1,0:T(8,128)(2,1)S(1)}, u32[]{:S(2)}) %copy-start.1) | copy-done | bytes 1048600
  89.8 3.6 %unpack.1 = bf16[8,2,256,128]{3,2,1,0:T(8,128)(2,1)} custom-call(f32[8,2,256,128]{3,2,1,0:T(8,128)} %near.1.near_ref, bf16[256,256]{1,0:T(8,128)(2,1)} %fusion.2.swap_ref, bf16[32,4,16,256]{3,2,1,0:T(8,128)(2,1)} %copy-done.1), custom_call_target="tpu_custom_call" | custom-call | tf_op jit(solution)/shard_map/unpack/pallas_call | solution.py:118
  (18 shorter events, 0.2 us)
Async XLA Ops:
  0.0 13.5 %copy-start.4 = (s32[2,256]{1,0:T(2,128)S(1)}, s32[2,256]{1,0:T(2,128)}, u32[]{:S(2)}) copy-start(s32[2,256]{1,0:T(2,128)} %mask_ref.1) | copy-start | bytes 6148
  0.0 14.7 %copy-start.5 = (f32[3,256]{1,0:T(4,128)S(1)}, f32[3,256]{1,0:T(4,128)}, u32[]{:S(2)}) copy-start(f32[3,256]{1,0:T(4,128)} %param.11) | copy-start | bytes 9220
  3.9 29.7 %all-to-all-start = ((bf16[32,4,16,256]{3,2,1,0:T(8,128)(2,1)}), bf16[32,4,16,256]{3,2,1,0:T(8,128)(2,1)S(1)}, u32[]{:S(2)}, u32[]{:S(2)}) async-start(bf16[32,4,16,256]{3,2,1,0:T(8,128)(2,1)} %pack.1), calls=%async_computation | async-start | bytes 2097152 | tf_op jit(solution)/shard_map/all_to_all | solution.py:255
  33.6 1.0 %copy-start = (bf16[32,4,16,256]{3,2,1,0:T(8,128)(2,1)}, bf16[32,4,16,256]{3,2,1,0:T(8,128)(2,1)S(1)}, u32[]{:S(2)}) copy-start(bf16[32,4,16,256]{3,2,1,0:T(8,128)(2,1)S(1)} %all-to-all-done.arrived_ref) | copy-start | bytes 3145732
  45.0 43.9 %all-to-all-start.1 = ((bf16[32,4,16,256]{3,2,1,0:T(8,128)(2,1)}), bf16[32,4,16,256]{3,2,1,0:T(8,128)(2,1)S(1)}, u32[]{:S(2)}, u32[]{:S(2)}) async-start(bf16[32,4,16,256]{3,2,1,0:T(8,128)(2,1)} %far.1), calls=%async_computation.1 | async-start | bytes 2097152 | tf_op jit(solution)/shard_map/all_to_all | solution.py:270
  52.6 26.6 %collective-permute-start = (bf16[1,2,256,128]{3,2,1,0:T(8,128)(2,1)S(1)}, bf16[1,2,256,128]{3,2,1,0:T(8,128)(2,1)S(1)}, u32[]{:S(2)}, u32[]{:S(2)}) collective-permute-start(bf16[1,2,256,128]{3,2,1,0:T(8,128)(2,1)S(1)} %get-tuple-element.8), channel_id=1, source_target_pairs={{0,1},{1,2},{2,3},{3,4},{4,5},{5,6},{6,7},{7,8},{8,9},{9,10},{10,1... | collective-permute-start | bytes 393224 | tf_op jit(solution)/shard_map/ppermute | solution.py:242
  55.7 23.5 %collective-permute-start.1 = (bf16[1,2,256,128]{3,2,1,0:T(8,128)(2,1)S(1)}, bf16[1,2,256,128]{3,2,1,0:T(8,128)(2,1)S(1)}, u32[]{:S(2)}, u32[]{:S(2)}) collective-permute-start(bf16[1,2,256,128]{3,2,1,0:T(8,128)(2,1)S(1)} %get-tuple-element.7), channel_id=1, source_target_pairs={{1,0},{2,1},{3,2},{4,3},{5,4},{6,5},{7,6},{8,7},{9,8},{10,9},{11,1... | collective-permute-start | bytes 393224 | tf_op jit(solution)/shard_map/ppermute | solution.py:243
  79.2 0.7 copy-start.2
  79.2 0.7 copy-start.3
  88.9 1.0 %copy-start.1 = (bf16[32,4,16,256]{3,2,1,0:T(8,128)(2,1)}, bf16[32,4,16,256]{3,2,1,0:T(8,128)(2,1)S(1)}, u32[]{:S(2)}) copy-start(bf16[32,4,16,256]{3,2,1,0:T(8,128)(2,1)S(1)} %all-to-all-done.1.refs_0_) | copy-start | bytes 3145732

commit v2 on v1

v2 whole, which is shorter than its diff:
```python
import functools
import math

import jax
import jax.numpy as jnp
from jax import lax
from jax.experimental import pallas as pl
from jax.experimental.pallas import tpu as pltpu
from jax.sharding import PartitionSpec as P


wave_number = 2.0
far_gain = 8.0
golden_turn = 2.399963229728653
axes = ("box", "dir")
chunks_wanted = 1
far_rows = 512
far_slots = 1
hbm = pl.BlockSpec(memory_space=pltpu.HBM)
vmem = pl.BlockSpec(memory_space=pltpu.VMEM)
params = pltpu.CompilerParams(vmem_limit_bytes=20 << 20)


def direction_cosines(count):
    order = jnp.arange(count, dtype=jnp.int32).astype(jnp.float32)
    height = 1.0 - (2.0 * order + 1.0) / count
    radial = jnp.sqrt(1.0 - height * height)
    azimuth = order * golden_turn
    return (radial * jnp.cos(azimuth), radial * jnp.sin(azimuth), height)


def phase_angles(points, count):
    dir_x, dir_y, dir_z = direction_cosines(count)
    return wave_number * (
        points[0][:, None] * dir_x[None, :]
        + points[1][:, None] * dir_y[None, :]
        + points[2][:, None] * dir_z[None, :]
    )


def far_matrix(centers, near_mask):
    total_boxes = centers.shape[1]
    squared = jnp.zeros((total_boxes, total_boxes), jnp.float32)
    for axis_number in range(3):
        spread = centers[axis_number][:, None] - centers[axis_number][None, :]
        squared = squared + spread * spread
    spacing = jnp.sqrt(1.0 + squared)
    kernel = jnp.cos(wave_number * spacing) / (1.0 + spacing) * (far_gain / math.sqrt(total_boxes))
    rows = jnp.arange(total_boxes, dtype=jnp.int32)[:, None]
    cols = jnp.arange(total_boxes, dtype=jnp.int32)[None, :]
    linked = (
        (cols == rows)
        | (cols == rows - 1) & (near_mask[0][:, None] == 1)
        | (cols == rows + 1) & (near_mask[1][:, None] == 1)
    )
    return jnp.where(linked, 0.0, kernel).astype(jnp.bfloat16)


def swap_matrix(outer, inner):
    size = outer * inner
    row = lax.broadcasted_iota(jnp.int32, (size, size), 0)
    col = lax.broadcasted_iota(jnp.int32, (size, size), 1)
    source = lax.rem(row, inner) * outer + lax.div(row, inner)
    return jnp.where(source == col, 1.0, 0.0).astype(jnp.bfloat16)


def held(value):
    return pltpu.with_memory_space_constraint(value, pltpu.VMEM)


def far_away(value):
    return pltpu.with_memory_space_constraint(value, pltpu.HBM)


def pack_body(currents_ref, *refs, devices, angles_each, group):
    outs, (loaded_ref, turned_ref, mixed_ref, load_sems, store_sems) = refs[:-5], refs[-5:]
    boxes, _, unknowns, angles = currents_ref.shape
    rows = 2 * boxes
    loads = [
        pltpu.make_async_copy(currents_ref.at[box], loaded_ref.at[box], load_sems.at[box])
        for box in range(boxes)
    ]
    for load in loads:
        load.start()
    swap = swap_matrix(group, rows)
    for box, load in enumerate(loads):
        load.wait()
        for part in range(2):
            turned_ref[part * boxes + box] = loaded_ref[box, part].T
    per_out = angles_each // len(outs)
    stores = []
    for number, first in enumerate(range(0, angles, group)):
        own, device = divmod(first, devices)
        tile = turned_ref[:, first : first + group, :].reshape(rows * group, unknowns)
        mixed = jnp.dot(swap, tile, preferred_element_type=jnp.float32)
        mixed_ref[number] = mixed.astype(jnp.bfloat16).reshape(group, rows, unknowns)
        which, slot = divmod(own, per_out)
        target = outs[which].at[pl.ds(device, group), slot]
        store = pltpu.make_async_copy(mixed_ref.at[number], target, store_sems.at[number])
        store.start()
        stores.append(store)
    for store in stores:
        store.wait()


def pack(currents, devices, chunks):
    boxes, _, unknowns, angles = currents.shape
    angles_each = angles // devices
    group = math.gcd(16, devices)
    rows = 2 * boxes
    body = functools.partial(pack_body, devices=devices, angles_each=angles_each, group=group)
    shape = jax.ShapeDtypeStruct((devices, angles_each // chunks, rows, unknowns), jnp.bfloat16)
    return pl.pallas_call(
        body,
        in_specs=[hbm],
        out_specs=[hbm] * chunks,
        out_shape=[shape] * chunks,
        scratch_shapes=[
            pltpu.VMEM(currents.shape, jnp.bfloat16),
            pltpu.VMEM((rows, angles, unknowns), jnp.bfloat16),
            pltpu.VMEM((angles // group, group, rows, unknowns), jnp.bfloat16),
            pltpu.SemaphoreType.DMA((boxes,)),
            pltpu.SemaphoreType.DMA((angles // group,)),
        ],
        compiler_params=params,
        name="pack",
    )(far_away(currents))


def unpack_body(near_ref, *refs, devices, angles_each, group):
    ins, (out_ref, loaded_ref, turned_ref, done_ref, load_sems, store_sems) = refs[:-6], refs[-6:]
    boxes, _, unknowns, angles = near_ref.shape
    rows = 2 * boxes
    per_in = angles_each // len(ins)
    loads = []
    for number, first in enumerate(range(0, angles, group)):
        own, device = divmod(first, devices)
        which, slot = divmod(own, per_in)
        source = ins[which].at[pl.ds(device, group), slot]
        loads.append(pltpu.make_async_copy(source, loaded_ref.at[number], load_sems.at[number]))
    for load in loads:
        load.start()
    swap = swap_matrix(rows, group)
    for number, load in enumerate(loads):
        load.wait()
        tile = loaded_ref[number].reshape(rows * group, unknowns)
        mixed = jnp.dot(swap, tile, preferred_element_type=jnp.float32)
        turned_ref[:, number * group : (number + 1) * group, :] = mixed.astype(
            jnp.bfloat16
        ).reshape(rows, group, unknowns)
    stores = [
        pltpu.make_async_copy(done_ref.at[box], out_ref.at[box], store_sems.at[box])
        for box in range(boxes)
    ]
    for box, store in enumerate(stores):
        for part in range(2):
            far = turned_ref[part * boxes + box].T.astype(jnp.float32)
            done_ref[box, part] = (near_ref[box, part] + far).astype(jnp.bfloat16)
        store.start()
    for store in stores:
        store.wait()


def unpack(near, pieces, devices):
    boxes, _, unknowns, angles = near.shape
    angles_each = angles // devices
    group = math.gcd(16, devices)
    rows = 2 * boxes
    body = functools.partial(unpack_body, devices=devices, angles_each=angles_each, group=group)
    return pl.pallas_call(
        body,
        in_specs=[vmem] + [hbm] * len(pieces),
        out_specs=hbm,
        out_shape=jax.ShapeDtypeStruct(near.shape, jnp.bfloat16),
        scratch_shapes=[
            pltpu.VMEM((angles // group, group, rows, unknowns), jnp.bfloat16),
            pltpu.VMEM((rows, angles, unknowns), jnp.bfloat16),
            pltpu.VMEM(near.shape, jnp.bfloat16),
            pltpu.SemaphoreType.DMA((angles // group,)),
            pltpu.SemaphoreType.DMA((boxes,)),
        ],
        compiler_params=params,
        name="unpack",
    )(held(near), *[far_away(x) for x in pieces])


def far_body(
    arrived_ref, gather_hbm, spread_hbm, translate_ref, cos_ref, sin_ref, out_ref,
    gather_ref, spread_ref, pat_ref, rec_ref, done_ref, load_sems, sems,
):
    devices, slots, rows, unknowns = arrived_ref.shape
    boxes = rows // 2
    total, count = cos_ref.shape
    width = math.gcd(count, 256)
    loads = []
    for number, low in enumerate(range(0, count, width)):
        piece = (slice(None), slice(None), pl.ds(low, width))
        loads.append(
            pltpu.make_async_copy(
                gather_hbm.at[piece], gather_ref.at[piece], load_sems.at[number]
            )
        )
    loads.append(pltpu.make_async_copy(spread_hbm, spread_ref, load_sems.at[len(loads)]))
    for load in loads:
        load.start()
    some = math.gcd(devices, max(1, far_rows // (slots * rows)))

    def product(left, right):
        return jnp.dot(left, right, preferred_element_type=jnp.float32)

    for number, low in enumerate(range(0, count, width)):
        high = low + width
        loads[number].wait()
        for first in range(0, devices, some):
            arrived = arrived_ref[first : first + some].reshape(some * slots * rows, unknowns)
            span = slice(first * boxes, (first + some) * boxes)
            shape = (some, slots, 2, boxes, width)
            by_re = product(arrived, gather_ref[0, :, low:high]).reshape(shape)
            by_im = product(arrived, gather_ref[1, :, low:high]).reshape(shape)
            cosine = cos_ref[span, low:high].reshape(some, boxes, width)
            sine = sin_ref[span, low:high].reshape(some, boxes, width)
            for slot in range(slots):
                pat_re = by_re[:, slot, 0] - by_im[:, slot, 1]
                pat_im = by_re[:, slot, 1] + by_im[:, slot, 0]
                out_re = (cosine * pat_re + sine * pat_im).reshape(some * boxes, width)
                out_im = (cosine * pat_im - sine * pat_re).reshape(some * boxes, width)
                pat_ref[slot, span, low:high] = out_re.astype(jnp.bfloat16)
                pat_ref[slot, span, count + low : count + high] = out_im.astype(jnp.bfloat16)
    loads[-1].wait()
    stores = []
    pairs = math.gcd(slots, far_slots)
    for begin in range(0, slots, pairs):
        for slot in range(begin, begin + pairs):
            for low in range(0, count, width):
                high = low + width
                translate = translate_ref[...]
                sum_re = product(translate, pat_ref[slot, :, low:high])
                sum_im = product(translate, pat_ref[slot, :, count + low : count + high])
                cosine = cos_ref[:, low:high]
                sine = sin_ref[:, low:high]
                rec_re = (cosine * sum_re - sine * sum_im).astype(jnp.bfloat16)
                rec_im = (cosine * sum_im + sine * sum_re).astype(jnp.bfloat16)
                rec_ref[slot, :, low:high] = rec_re
                rec_ref[slot, :, count + low : count + high] = rec_im
                rec_ref[slot, :, 2 * count + low : 2 * count + high] = -rec_re
        many = pairs * total
        whole = (pairs, devices, 1, boxes, unknowns)
        rec_re_im = rec_ref[begin : begin + pairs, :, : 2 * count].reshape(many, 2 * count)
        rec_im_re = rec_ref[begin : begin + pairs, :, count:].reshape(many, 2 * count)
        imag = product(rec_re_im, spread_ref[...]).reshape(whole)
        real = product(rec_im_re, spread_ref[...]).reshape(whole)
        both = jnp.concatenate([-real, imag], 2).reshape(pairs, devices, rows, unknowns)
        done_ref[begin : begin + pairs] = both.astype(jnp.bfloat16)
        for slot in range(begin, begin + pairs):
            store = pltpu.make_async_copy(done_ref.at[slot], out_ref.at[:, slot], sems.at[slot])
            store.start()
            stores.append(store)
    for store in stores:
        store.wait()


def far_field(arrived, gather, spread, translate, cosine, sine):
    devices, slots, rows, unknowns = arrived.shape
    total, count = cosine.shape
    return pl.pallas_call(
        far_body,
        in_specs=[vmem, hbm, hbm, vmem, vmem, vmem],
        out_specs=hbm,
        out_shape=jax.ShapeDtypeStruct(arrived.shape, jnp.bfloat16),
        scratch_shapes=[
            pltpu.VMEM(gather.shape, jnp.bfloat16),
            pltpu.VMEM(spread.shape, jnp.bfloat16),
            pltpu.VMEM((slots, total, 2 * count), jnp.bfloat16),
            pltpu.VMEM((slots, total, 3 * count), jnp.bfloat16),
            pltpu.VMEM((slots, devices, rows, unknowns), jnp.bfloat16),
            pltpu.SemaphoreType.DMA((1 + count // math.gcd(count, 256),)),
            pltpu.SemaphoreType.DMA((slots,)),
        ],
        compiler_params=params,
        name="far",
    )(held(arrived), far_away(gather), far_away(spread), *[held(x) for x in (translate, cosine, sine)])


def near_body(place_ref, mask_ref, currents_ref, low_ref, high_ref, blocks_ref, out_ref):
    boxes, _, unknowns, angles = currents_ref.shape
    box = pl.program_id(0)
    own = place_ref[0] * boxes + box

    def both(block):
        return jnp.concatenate([block[0], block[1]], 1)

    zero = jnp.zeros((unknowns, 2 * angles), jnp.bfloat16)
    here = both(currents_ref[box])
    before = jnp.where(box == 0, both(low_ref[0]), both(currents_ref[jnp.maximum(box - 1, 0)]))
    after = jnp.where(
        box == boxes - 1, both(high_ref[0]), both(currents_ref[jnp.minimum(box + 1, boxes - 1)])
    )
    before = jnp.where(mask_ref[0, own] == 1, before, zero)
    after = jnp.where(mask_ref[1, own] == 1, after, zero)
    by_re = jnp.zeros((unknowns, 2 * angles), jnp.float32)
    by_im = jnp.zeros((unknowns, 2 * angles), jnp.float32)
    for which, vectors in enumerate((here, before, after)):
        by_re += jnp.dot(blocks_ref[0, which, 0], vectors, preferred_element_type=jnp.float32)
        by_im += jnp.dot(blocks_ref[0, which, 1], vectors, preferred_element_type=jnp.float32)
    out_ref[box, 0] = by_re[:, :angles] - by_im[:, angles:]
    out_ref[box, 1] = by_re[:, angles:] + by_im[:, :angles]


def near_field(currents, low, high, near_blocks, near_mask, place):
    boxes, _, unknowns, _ = currents.shape
    return pl.pallas_call(
        near_body,
        grid_spec=pltpu.PrefetchScalarGridSpec(
            num_scalar_prefetch=2,
            grid=(boxes,),
            in_specs=[
                vmem,
                vmem,
                vmem,
                pl.BlockSpec((1, 3, 2, unknowns, unknowns), lambda i, *_: (i, 0, 0, 0, 0)),
            ],
            out_specs=vmem,
        ),
        out_shape=pltpu.VMEM(currents.shape, jnp.float32),
        compiler_params=params,
        name="near",
    )(place, near_mask, held(currents), held(low), held(high), near_blocks)


def edges(currents):
    count = lax.axis_size(axes)
    forward = [(i, i + 1) for i in range(count - 1)]
    backward = [(i + 1, i) for i in range(count - 1)]
    low = lax.ppermute(currents[-1:], axes, forward)
    high = lax.ppermute(currents[:1], axes, backward)
    return low, high


def exchange(value):
    return lax.all_to_all(value, axes, split_axis=0, concat_axis=0, tiled=True)


def product(currents, near_blocks, near_mask, aggregate, disaggregate, centers):
    devices = lax.axis_size(axes)
    angles_each = currents.shape[3] // devices
    chunks = math.gcd(chunks_wanted, angles_each)
    dir_count = aggregate.shape[1]
    place = lax.axis_index(axes).astype(jnp.int32).reshape(1)

    packed = pack(currents, devices, chunks)
    arrived = [exchange(x) for x in packed]
    low, high = edges(currents)
    gather = aggregate.transpose(0, 2, 1)
    turned = disaggregate.transpose(0, 2, 1)
    spread = jnp.concatenate([turned[1], turned[0]], 0)
    translate = far_matrix(centers, near_mask)
    theta = phase_angles(centers, dir_count)
    cosine = jnp.cos(theta)
    sine = jnp.sin(theta)
    far = [far_field(x, gather, spread, translate, cosine, sine) for x in arrived]
    pieces = [exchange(x) for x in far]
    near = near_field(currents, low, high, near_blocks, near_mask, place)
    return unpack(near, pieces, devices)


def solution(mesh):
    return jax.shard_map(
        product,
        mesh=mesh,
        in_specs=(
            P(axes, None, None, None),
            P(axes, None, None, None, None),
            P(),
            P(),
            P(),
            P(),
        ),
        out_specs=P(axes, None, None, None),
        check_vma=False,
    )
```

time: 94.3 us -> 83.3 us (0.88)
  Pallas kernels: 25.9 us -> 15.4 us
  other arithmetic: 7.45 us -> 4.35 us
  waiting for transfers between devices: 34 us -> 37 us
    pallas_call x1, Pallas kernels: 8.96 us -> 3.72 us  [near_field(): pl.pallas_call(near_body, grid_spec=pltpu.PrefetchScalarGridSpec(num_scal...]
    pallas_call x3, Pallas kernels: 16.9 us -> 11.7 us  [the longest x1 4.96 us: far_field(): pl.pallas_call(far_body, in_specs=[vmem, hbm, hbm, vmem, vmem, vmem], out...]
    all_to_all x2, waiting for transfers between devices: 13.6 us -> 15.7 us  [exchange(): return lax.all_to_all(value, axes, split_axis=0, concat_axis=0, tiled=True)]
    sin x1, other arithmetic: 3.18 us -> 2.01 us  [product(): sine = jnp.sin(theta)]
    another operation x2 -> x0, other arithmetic: 1.16 us -> none  [local(): jnp.stack([jnp.concatenate([turned[0], turned[1]], 1), jnp.concatenate([-...]
    slice x1, local copies, waits for them, and re-layouts: 0.99 us -> 0.02 us  [edges(): high = lax.ppermute(currents[:1], axes, backward)]
    unnamed x14 -> x10, local copies, waits for them, and re-layouts: 5.96 us -> 6.17 us
  transfers between devices with their start and end apart: 4 -> 4, of which waited for: 2 -> 2; matrix products, arithmetic and copies ran while one was open for 12% -> 9% of each run, Pallas kernels for 10% -> 4%
where the time goes in v2:
time: 83.3 us; the launch traced here: 82.8 us
  waiting for transfers between devices  37 us (44%)
  starting transfers between devices  19.7 us (24%)
  Pallas kernels  15.4 us (18%)
  local copies, waits for them, and re-layouts  6.23 us (7%)
  other arithmetic  4.35 us (5%)
    ppermute x1, waiting for transfers between devices, edges(): low = lax.ppermute(currents[-1:], axes, forward)  21.3 us
    all_to_all x2, waiting for transfers between devices, exchange(): return lax.all_to_all(value, axes, split_axis=0, concat_axis=0, tiled=True)  15.7 us
    all_to_all x2, starting transfers between devices, exchange(): return lax.all_to_all(value, axes, split_axis=0, concat_axis=0, tiled=True)  13.5 us
    unnamed x10, local copies, waits for them, and re-layouts  6.17 us
    pallas_call x1, Pallas kernels, far_field(): pl.pallas_call(far_body, in_specs=[vmem, hbm, hbm, vmem, vmem, vmem], out...  4.96 us
    pallas_call x1, Pallas kernels, unpack(): pl.pallas_call(body, in_specs=[vmem] + [hbm] * len(pieces), out_specs=hbm...  3.83 us
    pallas_call x1, Pallas kernels, near_field(): pl.pallas_call(near_body, grid_spec=pltpu.PrefetchScalarGridSpec(num_scal...  3.72 us
    ppermute x1, starting transfers between devices, edges(): low = lax.ppermute(currents[-1:], axes, forward)  3.11 us
  transfers between devices with their start and end apart: 4, of which 2 were waited for; matrix products, arithmetic and copies ran while one was open for 9% of the time, Pallas kernels for 4%

profile of v2, /device:TPU:17, one launch (start us, length us, event | category | flops | bytes accessed | tf_op | source)
XLA Modules:
  0.0 82.8 jit_solution(6547521908068992668)
XLA Ops:
  0.0 0.0 copy-start.2
  0.0 0.0 copy-start.3
  0.0 2.9 %pack.1 = bf16[32,4,16,256]{3,2,1,0:T(8,128)(2,1)} custom-call(bf16[8,2,256,128]{3,2,1,0:T(8,128)(2,1)} %currents_ref.3), custom_call_target="tpu_custom_call" | custom-call | tf_op jit(solution)/shard_map/pack/pallas_call | solution.py:113
  2.9 6.2 %all-to-all-start = ((bf16[32,4,16,256]{3,2,1,0:T(8,128)(2,1)}), bf16[32,4,16,256]{3,2,1,0:T(8,128)(2,1)S(1)}, u32[]{:S(2)}, u32[]{:S(2)}) async-start(bf16[32,4,16,256]{3,2,1,0:T(8,128)(2,1)} %pack.1), calls=%async_computation | async-start | bytes 2097152 | tf_op jit(solution)/shard_map/all_to_all | solution.py:340
  9.2 0.0 copy-start.1
  9.2 1.3 %copy.8 = bf16[2,256,512]{1,2,0:T(8,128)(2,1)S(1)} copy(bf16[2,256,512]{2,1,0:T(8,128)(2,1)} %param.10) | data formatting | bytes 1048576 | tf_op args[4]
  10.5 2.0 %copy.7 = bf16[2,512,256]{1,2,0:T(8,128)(2,1)} copy(bf16[2,512,256]{2,1,0:T(8,128)(2,1)} %param.9) | data formatting | bytes 1048576 | tf_op args[3]
  12.6 0.0 copy-done.2
  12.7 0.8 pad_maximum_fusion.spread_hbm
  13.5 0.0 copy-done.3
  13.5 1.4 %select_convert_fusion.translate_ref = bf16[256,256]{1,0:T(8,128)(2,1)S(1)} fusion(f32[256]{0:T(256)S(1)} %bitcast.14, f32[256]{0:T(256)S(1)} %bitcast.16, f32[256]{0:T(256)S(1)} %bitcast.12, s32[256]{0:T(256)S(1)} %get-tuple-element.16, s32[256]{0:T(256)S(1)} %get-tuple-element.17, pred[256]{0:T(512)(128)(4,1)S(1)} %get-tuple-element.6, ...), kind=kLoop, calls=%fused_computation.6 | loop fusion | flops 1441792 | bytes 136704 | tf_op jit(solution)/shard_map/convert_element_type | solution.py:56
  15.0 2.0 %fusion = (f32[256,512]{1,0:T(8,128)S(1)}, f32[256,512]{1,0:T(8,128)S(1)}) fusion(f32[512]{0:T(512)S(1)} %multiply_subtract_fusion, f32[256]{0:T(256)S(1)} %bitcast.15, f32[512]{0:T(512)S(1)} %get-tuple-element.18, f32[256]{0:T(256)S(1)} %bitcast.17, f32[512]{0:T(512)S(1)} %get-tuple-element.19, f32[256]{0:T(256)S(1)} %bitcast.13), kind=kLoop, calls=%fused_computation.2 | loop fusion | flops 786432 | bytes 1057792 | tf_op jit(solution)/shard_map/sin | solution.py:359
  17.0 15.7 %all-to-all-done.arrived_ref = bf16[32,4,16,256]{3,2,1,0:T(8,128)(2,1)S(1)} async-done(((bf16[32,4,16,256]{3,2,1,0:T(8,128)(2,1)}), bf16[32,4,16,256]{3,2,1,0:T(8,128)(2,1)S(1)}, u32[]{:S(2)}, u32[]{:S(2)}) %all-to-all-start) | async-done | bytes 1048608 | tf_op jit(solution)/shard_map/all_to_all | solution.py:340
  32.7 5.0 %far.1 = bf16[32,4,16,256]{3,2,1,0:T(8,128)(2,1)} custom-call(bf16[32,4,16,256]{3,2,1,0:T(8,128)(2,1)S(1)} %all-to-all-done.arrived_ref, bf16[2,256,512]{2,1,0:T(8,128)(2,1)} %bitcast.10, bf16[1024,256]{1,0:T(8,128)(2,1)} %pad_maximum_fusion.spread_hbm, bf16[256,256]{1,0:T(8,128)(2,1)S(1)} %select_convert_fusion.translate_ref, ...), custom_call_target="tpu_custom_call" | custom-call | tf_op jit(solution)/shard_map/far/pallas_call | solution.py:265
  37.6 7.3 %all-to-all-start.1 = ((bf16[32,4,16,256]{3,2,1,0:T(8,128)(2,1)}), bf16[32,4,16,256]{3,2,1,0:T(8,128)(2,1)}, u32[]{:S(2)}, u32[]{:S(2)}) async-start(bf16[32,4,16,256]{3,2,1,0:T(8,128)(2,1)} %far.1), calls=%async_computation.1 | async-start | bytes 2097152 | tf_op jit(solution)/shard_map/all_to_all | solution.py:340
  44.9 0.0 copy-done.1
  44.9 3.1 %collective-permute-start = (bf16[1,2,256,128]{3,2,1,0:T(8,128)(2,1)S(1)}, bf16[1,2,256,128]{3,2,1,0:T(8,128)(2,1)S(1)}, u32[]{:S(2)}, u32[]{:S(2)}) collective-permute-start(bf16[1,2,256,128]{3,2,1,0:T(8,128)(2,1)S(1)} %get-tuple-element.8), channel_id=1, source_target_pairs={{0,1},{1,2},{2,3},{3,4},{4,5},{5,6},{6,7},{7,8},{8,9},{9,10},{10,1... | collective-permute-start | bytes 393224 | tf_op jit(solution)/shard_map/ppermute | solution.py:334
  48.1 3.1 %collective-permute-start.1 = (bf16[1,2,256,128]{3,2,1,0:T(8,128)(2,1)S(1)}, bf16[1,2,256,128]{3,2,1,0:T(8,128)(2,1)S(1)}, u32[]{:S(2)}, u32[]{:S(2)}) collective-permute-start(bf16[1,2,256,128]{3,2,1,0:T(8,128)(2,1)S(1)} %get-tuple-element.7), channel_id=1, source_target_pairs={{1,0},{2,1},{3,2},{4,3},{5,4},{6,5},{7,6},{8,7},{9,8},{10,9},{11,1... | collective-permute-start | bytes 393224 | tf_op jit(solution)/shard_map/ppermute | solution.py:335
  51.1 21.3 %collective-permute-done.low_ref = bf16[1,2,256,128]{3,2,1,0:T(8,128)(2,1)S(1)} collective-permute-done((bf16[1,2,256,128]{3,2,1,0:T(8,128)(2,1)S(1)}, bf16[1,2,256,128]{3,2,1,0:T(8,128)(2,1)S(1)}, u32[]{:S(2)}, u32[]{:S(2)}) %collective-permute-start) | collective-permute-done | bytes 131104 | tf_op jit(solution)/shard_map/ppermute | solution.py:334
  72.5 0.0 collective-permute-done.1.high_ref
  72.5 2.8 %copy-done = bf16[8,3,2,256,256]{4,3,2,1,0:T(8,128)(2,1)S(1)} copy-done((bf16[8,3,2,256,256]{4,3,2,1,0:T(8,128)(2,1)S(1)}, bf16[8,3,2,256,256]{4,3,2,1,0:T(8,128)(2,1)}, u32[]{:S(2)}) %copy-start) | copy-done | bytes 6291480
  75.3 3.7 %near.1.near_ref = f32[8,2,256,128]{3,2,1,0:T(8,128)S(1)} custom-call(s32[1]{0:T(128)} %bitcast.place_ref, s32[2,256]{1,0:T(2,128)S(1)} %copy-done.2, bf16[8,2,256,128]{3,2,1,0:T(8,128)(2,1)S(1)} %copy-done.1, bf16[1,2,256,128]{3,2,1,0:T(8,128)(2,1)S(1)} %collective-permute-done.low_ref, bf16[1,2,256,128]{3,2,1,0:T(8,128)(2,1)S(1)} %collective-permute-done.1.high_ref, ...), custom_call_target="tpu_custom_call" | custom-call | tf_op jit(solution)/shard_map/near/pallas_call | solution.py:311
  79.0 0.0 all-to-all-done.1.refs_0_
  79.0 3.8 %unpack.1 = bf16[8,2,256,128]{3,2,1,0:T(8,128)(2,1)} custom-call(f32[8,2,256,128]{3,2,1,0:T(8,128)S(1)} %near.1.near_ref, bf16[32,4,16,256]{3,2,1,0:T(8,128)(2,1)} %all-to-all-done.1.refs_0_), custom_call_target="tpu_custom_call" | custom-call | tf_op jit(solution)/shard_map/unpack/pallas_call | solution.py:170
  (8 shorter events, 0.1 us)
Async XLA Ops:
  0.0 12.6 %copy-start.2 = (s32[2,256]{1,0:T(2,128)S(1)}, s32[2,256]{1,0:T(2,128)}, u32[]{:S(2)}) copy-start(s32[2,256]{1,0:T(2,128)} %mask_ref.1) | copy-start | bytes 6148
  0.0 13.5 %copy-start.3 = (f32[3,256]{1,0:T(4,128)S(1)}, f32[3,256]{1,0:T(4,128)}, u32[]{:S(2)}) copy-start(f32[3,256]{1,0:T(4,128)} %param.11) | copy-start | bytes 9220
  2.9 29.7 %all-to-all-start = ((bf16[32,4,16,256]{3,2,1,0:T(8,128)(2,1)}), bf16[32,4,16,256]{3,2,1,0:T(8,128)(2,1)S(1)}, u32[]{:S(2)}, u32[]{:S(2)}) async-start(bf16[32,4,16,256]{3,2,1,0:T(8,128)(2,1)} %pack.1), calls=%async_computation | async-start | bytes 2097152 | tf_op jit(solution)/shard_map/all_to_all | solution.py:340
  9.2 35.7 %copy-start.1 = (bf16[8,2,256,128]{3,2,1,0:T(8,128)(2,1)S(1)}, bf16[8,2,256,128]{3,2,1,0:T(8,128)(2,1)}, u32[]{:S(2)}) copy-start(bf16[8,2,256,128]{3,2,1,0:T(8,128)(2,1)} %currents_ref.3) | copy-start | bytes 3145732
  37.6 41.4 %all-to-all-start.1 = ((bf16[32,4,16,256]{3,2,1,0:T(8,128)(2,1)}), bf16[32,4,16,256]{3,2,1,0:T(8,128)(2,1)}, u32[]{:S(2)}, u32[]{:S(2)}) async-start(bf16[32,4,16,256]{3,2,1,0:T(8,128)(2,1)} %far.1), calls=%async_computation.1 | async-start | bytes 2097152 | tf_op jit(solution)/shard_map/all_to_all | solution.py:340
  44.9 27.5 %collective-permute-start = (bf16[1,2,256,128]{3,2,1,0:T(8,128)(2,1)S(1)}, bf16[1,2,256,128]{3,2,1,0:T(8,128)(2,1)S(1)}, u32[]{:S(2)}, u32[]{:S(2)}) collective-permute-start(bf16[1,2,256,128]{3,2,1,0:T(8,128)(2,1)S(1)} %get-tuple-element.8), channel_id=1, source_target_pairs={{0,1},{1,2},{2,3},{3,4},{4,5},{5,6},{6,7},{7,8},{8,9},{9,10},{10,1... | collective-permute-start | bytes 393224 | tf_op jit(solution)/shard_map/ppermute | solution.py:334
  48.1 24.4 %collective-permute-start.1 = (bf16[1,2,256,128]{3,2,1,0:T(8,128)(2,1)S(1)}, bf16[1,2,256,128]{3,2,1,0:T(8,128)(2,1)S(1)}, u32[]{:S(2)}, u32[]{:S(2)}) collective-permute-start(bf16[1,2,256,128]{3,2,1,0:T(8,128)(2,1)S(1)} %get-tuple-element.7), channel_id=1, source_target_pairs={{1,0},{2,1},{3,2},{4,3},{5,4},{6,5},{7,6},{8,7},{9,8},{10,9},{11,1... | collective-permute-start | bytes 393224 | tf_op jit(solution)/shard_map/ppermute | solution.py:335
  72.5 2.8 %copy-start = (bf16[8,3,2,256,256]{4,3,2,1,0:T(8,128)(2,1)S(1)}, bf16[8,3,2,256,256]{4,3,2,1,0:T(8,128)(2,1)}, u32[]{:S(2)}) copy-start(bf16[8,3,2,256,256]{4,3,2,1,0:T(8,128)(2,1)} %blocks_ref.1) | copy-start | bytes 18874372

commit v3 on v2

--- a/solution.py
+++ b/solution.py
@@ -6,15 +6,17 @@
 from jax import lax
 from jax.experimental import pallas as pl
 from jax.experimental.pallas import tpu as pltpu
-from jax.sharding import PartitionSpec as P
+from jax.sharding import Mesh, PartitionSpec as P
 
 
 wave_number = 2.0
 far_gain = 8.0
 golden_turn = 2.399963229728653
-axes = ("box", "dir")
+axes = ("outer", "core", "far", "close")
+route = ("outer", "close", "core", "far")
 chunks_wanted = 1
 far_rows = 512
+pack_waits = 4
 far_slots = 1
 hbm = pl.BlockSpec(memory_space=pltpu.HBM)
 vmem = pl.BlockSpec(memory_space=pltpu.VMEM)
@@ -38,7 +40,7 @@
     )
 
 
-def far_matrix(centers, near_mask):
+def far_matrix(centers, near_mask, names):
     total_boxes = centers.shape[1]
     squared = jnp.zeros((total_boxes, total_boxes), jnp.float32)
     for axis_number in range(3):
@@ -46,8 +48,8 @@
         squared = squared + spread * spread
     spacing = jnp.sqrt(1.0 + squared)
     kernel = jnp.cos(wave_number * spacing) / (1.0 + spacing) * (far_gain / math.sqrt(total_boxes))
-    rows = jnp.arange(total_boxes, dtype=jnp.int32)[:, None]
-    cols = jnp.arange(total_boxes, dtype=jnp.int32)[None, :]
+    rows = names[:, None]
+    cols = names[None, :]
     linked = (
         (cols == rows)
         | (cols == rows - 1) & (near_mask[0][:, None] == 1)
@@ -83,8 +85,10 @@
     for load in loads:
         load.start()
     swap = swap_matrix(group, rows)
-    for box, load in enumerate(loads):
-        load.wait()
+    for box in range(boxes):
+        if box % pack_waits == 0:
+            for load in loads[box : box + pack_waits]:
+                load.wait()
         for part in range(2):
             turned_ref[part * boxes + box] = loaded_ref[box, part].T
     per_out = angles_each // len(outs)
@@ -128,34 +132,28 @@
 
 
 def unpack_body(near_ref, *refs, devices, angles_each, group):
-    ins, (out_ref, loaded_ref, turned_ref, done_ref, load_sems, store_sems) = refs[:-6], refs[-6:]
+    ins, (out_ref, turned_ref, done_ref, sems) = refs[:-4], refs[-4:]
     boxes, _, unknowns, angles = near_ref.shape
     rows = 2 * boxes
     per_in = angles_each // len(ins)
-    loads = []
-    for number, first in enumerate(range(0, angles, group)):
+    swap = swap_matrix(rows, group)
+    for first in range(0, angles, group):
         own, device = divmod(first, devices)
         which, slot = divmod(own, per_in)
-        source = ins[which].at[pl.ds(device, group), slot]
-        loads.append(pltpu.make_async_copy(source, loaded_ref.at[number], load_sems.at[number]))
-    for load in loads:
-        load.start()
-    swap = swap_matrix(rows, group)
-    for number, load in enumerate(loads):
-        load.wait()
-        tile = loaded_ref[number].reshape(rows * group, unknowns)
+        tile = ins[which][device : device + group, slot].reshape(rows * group, unknowns)
         mixed = jnp.dot(swap, tile, preferred_element_type=jnp.float32)
-        turned_ref[:, number * group : (number + 1) * group, :] = mixed.astype(
-            jnp.bfloat16
-        ).reshape(rows, group, unknowns)
+        turned_ref[:, first : first + group, :] = mixed.astype(jnp.bfloat16).reshape(
+            rows, group, unknowns
+        )
     stores = [
-        pltpu.make_async_copy(done_ref.at[box], out_ref.at[box], store_sems.at[box])
+        pltpu.make_async_copy(done_ref.at[box], out_ref.at[box], sems.at[box])
         for box in range(boxes)
     ]
     for box, store in enumerate(stores):
         for part in range(2):
             far = turned_ref[part * boxes + box].T.astype(jnp.float32)
-            done_ref[box, part] = (near_ref[box, part] + far).astype(jnp.bfloat16)
+            near = near_ref[box, part].astype(jnp.float32)
+            done_ref[box, part] = (near + far).astype(jnp.bfloat16)
         store.start()
     for store in stores:
         store.wait()
@@ -169,54 +167,48 @@
     body = functools.partial(unpack_body, devices=devices, angles_each=angles_each, group=group)
     return pl.pallas_call(
         body,
-        in_specs=[vmem] + [hbm] * len(pieces),
+        in_specs=[vmem] * (1 + len(pieces)),
         out_specs=hbm,
         out_shape=jax.ShapeDtypeStruct(near.shape, jnp.bfloat16),
         scratch_shapes=[
-            pltpu.VMEM((angles // group, group, rows, unknowns), jnp.bfloat16),
             pltpu.VMEM((rows, angles, unknowns), jnp.bfloat16),
             pltpu.VMEM(near.shape, jnp.bfloat16),
-            pltpu.SemaphoreType.DMA((angles // group,)),
             pltpu.SemaphoreType.DMA((boxes,)),
         ],
         compiler_params=params,
         name="unpack",
-    )(held(near), *[far_away(x) for x in pieces])
+    )(held(near), *[held(x) for x in pieces])
 
 
 def far_body(
-    arrived_ref, gather_hbm, spread_hbm, translate_ref, cos_ref, sin_ref, out_ref,
-    gather_ref, spread_ref, pat_ref, rec_ref, done_ref, load_sems, sems,
+    arrived_ref, gather_ref, gather_hbm, spread_hbm, translate_ref, cos_ref, sin_ref, out_ref,
+    later_ref, spread_ref, pat_ref, rec_ref, done_ref, later_sem, load_sem, sems,
 ):
     devices, slots, rows, unknowns = arrived_ref.shape
     boxes = rows // 2
     total, count = cos_ref.shape
-    width = math.gcd(count, 256)
-    loads = []
-    for number, low in enumerate(range(0, count, width)):
-        piece = (slice(None), slice(None), pl.ds(low, width))
-        loads.append(
-            pltpu.make_async_copy(
-                gather_hbm.at[piece], gather_ref.at[piece], load_sems.at[number]
-            )
-        )
-    loads.append(pltpu.make_async_copy(spread_hbm, spread_ref, load_sems.at[len(loads)]))
-    for load in loads:
-        load.start()
+    width = gather_ref.shape[2]
+    later = pltpu.make_async_copy(gather_hbm, later_ref, later_sem)
+    later.start()
+    load = pltpu.make_async_copy(spread_hbm, spread_ref, load_sem)
+    load.start()
     some = math.gcd(devices, max(1, far_rows // (slots * rows)))
 
     def product(left, right):
         return jnp.dot(left, right, preferred_element_type=jnp.float32)
 
-    for number, low in enumerate(range(0, count, width)):
+    for low in range(0, count, width):
         high = low + width
-        loads[number].wait()
+        table_ref = later_ref if low else gather_ref
+        start = max(0, low - width)
+        if low == width:
+            later.wait()
         for first in range(0, devices, some):
             arrived = arrived_ref[first : first + some].reshape(some * slots * rows, unknowns)
             span = slice(first * boxes, (first + some) * boxes)
             shape = (some, slots, 2, boxes, width)
-            by_re = product(arrived, gather_ref[0, :, low:high]).reshape(shape)
-            by_im = product(arrived, gather_ref[1, :, low:high]).reshape(shape)
+            by_re = product(arrived, table_ref[0, :, start : start + width]).reshape(shape)
+            by_im = product(arrived, table_ref[1, :, start : start + width]).reshape(shape)
             cosine = cos_ref[span, low:high].reshape(some, boxes, width)
             sine = sin_ref[span, low:high].reshape(some, boxes, width)
             for slot in range(slots):
@@ -226,7 +218,7 @@
                 out_im = (cosine * pat_im - sine * pat_re).reshape(some * boxes, width)
                 pat_ref[slot, span, low:high] = out_re.astype(jnp.bfloat16)
                 pat_ref[slot, span, count + low : count + high] = out_im.astype(jnp.bfloat16)
-    loads[-1].wait()
+    load.wait()
     stores = []
     pairs = math.gcd(slots, far_slots)
     for begin in range(0, slots, pairs):
@@ -262,23 +254,26 @@
 def far_field(arrived, gather, spread, translate, cosine, sine):
     devices, slots, rows, unknowns = arrived.shape
     total, count = cosine.shape
+    width = math.gcd(count // 2, 256)
+    later = gather[:, :, width:]
     return pl.pallas_call(
         far_body,
-        in_specs=[vmem, hbm, hbm, vmem, vmem, vmem],
+        in_specs=[vmem, vmem, hbm, hbm, vmem, vmem, vmem],
         out_specs=hbm,
         out_shape=jax.ShapeDtypeStruct(arrived.shape, jnp.bfloat16),
         scratch_shapes=[
-            pltpu.VMEM(gather.shape, jnp.bfloat16),
+            pltpu.VMEM(later.shape, jnp.bfloat16),
             pltpu.VMEM(spread.shape, jnp.bfloat16),
             pltpu.VMEM((slots, total, 2 * count), jnp.bfloat16),
             pltpu.VMEM((slots, total, 3 * count), jnp.bfloat16),
             pltpu.VMEM((slots, devices, rows, unknowns), jnp.bfloat16),
-            pltpu.SemaphoreType.DMA((1 + count // math.gcd(count, 256),)),
+            pltpu.SemaphoreType.DMA(()),
+            pltpu.SemaphoreType.DMA(()),
             pltpu.SemaphoreType.DMA((slots,)),
         ],
         compiler_params=params,
         name="far",
-    )(held(arrived), far_away(gather), far_away(spread), *[held(x) for x in (translate, cosine, sine)])
+    )(held(arrived), held(gather[:, :, :width]), far_away(later), far_away(spread), *[held(x) for x in (translate, cosine, sine)])
 
 
 def near_body(place_ref, mask_ref, currents_ref, low_ref, high_ref, blocks_ref, out_ref):
@@ -302,8 +297,8 @@
     for which, vectors in enumerate((here, before, after)):
         by_re += jnp.dot(blocks_ref[0, which, 0], vectors, preferred_element_type=jnp.float32)
         by_im += jnp.dot(blocks_ref[0, which, 1], vectors, preferred_element_type=jnp.float32)
-    out_ref[box, 0] = by_re[:, :angles] - by_im[:, angles:]
-    out_ref[box, 1] = by_re[:, angles:] + by_im[:, :angles]
+    out_ref[box, 0] = (by_re[:, :angles] - by_im[:, angles:]).astype(jnp.bfloat16)
+    out_ref[box, 1] = (by_re[:, angles:] + by_im[:, :angles]).astype(jnp.bfloat16)
 
 
 def near_field(currents, low, high, near_blocks, near_mask, place):
@@ -321,23 +316,31 @@
             ],
             out_specs=vmem,
         ),
-        out_shape=pltpu.VMEM(currents.shape, jnp.float32),
+        out_shape=pltpu.VMEM(currents.shape, jnp.bfloat16),
         compiler_params=params,
         name="near",
-    )(place, near_mask, held(currents), held(low), held(high), near_blocks)
+    )(place, near_mask, currents, low, high, near_blocks)
 
 
 def edges(currents):
     count = lax.axis_size(axes)
     forward = [(i, i + 1) for i in range(count - 1)]
     backward = [(i + 1, i) for i in range(count - 1)]
-    low = lax.ppermute(currents[-1:], axes, forward)
-    high = lax.ppermute(currents[:1], axes, backward)
+    low = lax.ppermute(far_away(currents[-1:]), axes, forward)
+    high = lax.ppermute(far_away(currents[:1]), axes, backward)
     return low, high
 
 
+def routed(values):
+    sizes = [lax.axis_size(axis) for axis in axes]
+    split = values.reshape(values.shape[:-1] + (*sizes, -1))
+    lead = values.ndim - 1
+    order = [*range(lead), *(lead + axes.index(axis) for axis in route), lead + len(axes)]
+    return split.transpose(order).reshape(values.shape)
+
+
 def exchange(value):
-    return lax.all_to_all(value, axes, split_axis=0, concat_axis=0, tiled=True)
+    return lax.all_to_all(value, route, split_axis=0, concat_axis=0, tiled=True)
 
 
 def product(currents, near_blocks, near_mask, aggregate, disaggregate, centers):
@@ -353,8 +356,10 @@
     gather = aggregate.transpose(0, 2, 1)
     turned = disaggregate.transpose(0, 2, 1)
     spread = jnp.concatenate([turned[1], turned[0]], 0)
-    translate = far_matrix(centers, near_mask)
-    theta = phase_angles(centers, dir_count)
+    names = jnp.arange(centers.shape[1], dtype=jnp.int32)
+    points = routed(centers)
+    translate = far_matrix(points, routed(near_mask), routed(names))
+    theta = phase_angles(points, dir_count)
     cosine = jnp.cos(theta)
     sine = jnp.sin(theta)
     far = [far_field(x, gather, spread, translate, cosine, sine) for x in arrived]
@@ -364,9 +369,14 @@
 
 
 def solution(mesh):
+    box, direction = (mesh.shape[axis] for axis in ("box", "dir"))
+    core = math.gcd(box, 2)
+    close = math.gcd(direction, 2)
+    shape = (box // core, core, direction // close, close)
+    finer = Mesh(mesh.devices.reshape(shape), axes)
     return jax.shard_map(
         product,
-        mesh=mesh,
+        mesh=finer,
         in_specs=(
             P(axes, None, None, None),
             P(axes, None, None, None, None),

time: 83.3 us -> 80.7 us (0.969)
  local copies, waits for them, and re-layouts: 6.23 us -> 9.08 us
  starting transfers between devices: 19.7 us -> 17 us
  Pallas kernels: 15.4 us -> 13.4 us
  waiting for transfers between devices: 37 us -> 35.9 us
    pallas_call x2, Pallas kernels: 8.79 us -> 5.93 us  [the longest x1 4.29 us: far_field(): pl.pallas_call(far_body, in_specs=[vmem, vmem, hbm, hbm, vmem, vmem, vmem...]
    all_to_all x2, starting transfers between devices: 13.5 us -> 10.9 us  [exchange(): return lax.all_to_all(value, route, split_axis=0, concat_axis=0, tiled=True)]
    reshape x0 -> x5, local copies, waits for them, and re-layouts: none -> 1.72 us  [routed(): split = values.reshape(values.shape[:-1] + (*sizes, -1))]
    pallas_call x1, Pallas kernels: 3.72 us -> 4.66 us  [near_field(): pl.pallas_call(near_body, grid_spec=pltpu.PrefetchScalarGridSpec(num_scal...]
    all_to_all x2, waiting for transfers between devices: 15.7 us -> 14.8 us  [exchange(): return lax.all_to_all(value, route, split_axis=0, concat_axis=0, tiled=True)]
    unnamed x10 -> x12, local copies, waits for them, and re-layouts: 6.17 us -> 6.09 us
  transfers between devices with their start and end apart: 4 -> 4, of which waited for: 2 -> 2; matrix products, arithmetic and copies ran while one was open for 9% -> 12% of each run, Pallas kernels for 4% -> 6%
where the time goes in v3:
time: 80.7 us; the launch traced here: 79.9 us
  waiting for transfers between devices  35.9 us (44%)
  starting transfers between devices  17 us (21%)
  Pallas kernels  13.4 us (17%)
  local copies, waits for them, and re-layouts  9.08 us (11%)
  other arithmetic  4.34 us (5%)
    ppermute x1, waiting for transfers between devices, edges(): low = lax.ppermute(far_away(currents[-1:]), axes, forward)  21.1 us
    all_to_all x2, waiting for transfers between devices, exchange(): return lax.all_to_all(value, route, split_axis=0, concat_axis=0, tiled=True)  14.8 us
    all_to_all x2, starting transfers between devices, exchange(): return lax.all_to_all(value, route, split_axis=0, concat_axis=0, tiled=True)  10.9 us
    unnamed x12, local copies, waits for them, and re-layouts  6.09 us
    pallas_call x1, Pallas kernels, near_field(): pl.pallas_call(near_body, grid_spec=pltpu.PrefetchScalarGridSpec(num_scal...  4.66 us
    pallas_call x1, Pallas kernels, far_field(): pl.pallas_call(far_body, in_specs=[vmem, vmem, hbm, hbm, vmem, vmem, vmem...  4.29 us
    ppermute x1, starting transfers between devices, edges(): low = lax.ppermute(far_away(currents[-1:]), axes, forward)  3.1 us
    ppermute x1, starting transfers between devices, edges(): high = lax.ppermute(far_away(currents[:1]), axes, backward)  3.09 us
  transfers between devices with their start and end apart: 4, of which 2 were waited for; matrix products, arithmetic and copies ran while one was open for 12% of the time, Pallas kernels for 6%

profile of v3, /device:TPU:17, one launch (start us, length us, event | category | flops | bytes accessed | tf_op | source)
XLA Modules:
  0.0 79.9 jit_solution(9204306129485036067)
XLA Ops:
  0.0 2.8 %pack.1 = bf16[32,4,16,256]{3,2,1,0:T(8,128)(2,1)} custom-call(bf16[8,2,256,128]{3,2,1,0:T(8,128)(2,1)} %currents_ref.3), custom_call_target="tpu_custom_call" | custom-call | tf_op jit(solution)/shard_map/pack/pallas_call | solution.py:117
  2.8 6.2 %all-to-all-start = ((bf16[32,4,16,256]{3,2,1,0:T(8,128)(2,1)}), bf16[32,4,16,256]{3,2,1,0:T(8,128)(2,1)S(1)}, u32[]{:S(2)}, u32[]{:S(2)}) async-start(bf16[32,4,16,256]{3,2,1,0:T(8,128)(2,1)} %pack.1), calls=%async_computation | async-start | bytes 2097152 | tf_op jit(solution)/shard_map/all_to_all | solution.py:343
  9.0 0.8 %reshape.283 = f32[3,2,2,4,2,8]{5,4,3,2,1,0:T(2,128)S(1)} reshape(f32[3,256]{1,0:T(4,128)} %param.11) | data formatting | bytes 6144 | tf_op jit(solution)/shard_map/reshape | solution.py:336
  9.9 0.1 sub.82
  10.0 0.1 sub.86
  10.3 0.8 reshape.282
  11.1 0.1 eq.67
  11.2 0.1 eq.71
  11.3 1.3 %copy.10 = bf16[2,256,512]{1,2,0:T(8,128)(2,1)S(1)} copy(bf16[2,256,512]{2,1,0:T(8,128)(2,1)} %param.10) | data formatting | bytes 1048576 | tf_op args[4]
  12.6 1.3 %copy.9 = bf16[2,512,256]{1,2,0:T(8,128)(2,1)S(1)} copy(bf16[2,512,256]{2,1,0:T(8,128)(2,1)} %param.9) | data formatting | bytes 1048576 | tf_op args[3]
  14.0 0.8 %pad_maximum_fusion.spread_hbm = bf16[1024,256]{1,0:T(8,128)(2,1)} fusion(bf16[512,256]{1,0:T(8,128)(2,1)S(1)} %get-tuple-element.8, bf16[512,256]{1,0:T(8,128)(2,1)S(1)} %get-tuple-element.7), kind=kLoop, calls=%fused_computation | loop fusion | flops 1048576 | bytes 1048576 | tf_op jit(solution)/shard_map/concatenate | solution.py:358
  14.9 1.4 %select_convert_fusion.translate_ref = bf16[256,256]{1,0:T(8,128)(2,1)S(1)} fusion(f32[256]{0:T(256)S(1)} %sub.86, f32[256]{0:T(256)S(1)} %sub.82, f32[256]{0:T(256)S(1)} %sub.78, s32[256]{0:T(256)S(1)} %reshape.285, s32[256]{0:T(256)S(1)} %get-tuple-element.19, s32[256]{0:T(256)S(1)} %get-tuple-element.18, pred[256]{0:T(512)(128)(4,1)S(1)} %eq.71, ...), kind=kLoop, calls=%fused_computation.6 | loop fusion | flops 1441792 | bytes 137728 | tf_op jit(solution)/shard_map/convert_element_type | solution.py:58
  16.3 0.7 fusion.3
  17.0 2.0 %fusion = (f32[256,512]{1,0:T(8,128)S(1)}, f32[256,512]{1,0:T(8,128)S(1)}) fusion(f32[512]{0:T(512)S(1)} %multiply_subtract_fusion, f32[256]{0:T(256)S(1)} %sub.86, f32[512]{0:T(512)S(1)} %get-tuple-element.20, f32[256]{0:T(256)S(1)} %sub.82, f32[512]{0:T(512)S(1)} %get-tuple-element.21, f32[256]{0:T(256)S(1)} %sub.78), kind=kLoop, calls=%fused_computation.2 | loop fusion | flops 786432 | bytes 1057792 | tf_op jit(solution)/shard_map/sin | solution.py:364
  19.0 14.8 %all-to-all-done.arrived_ref = bf16[32,4,16,256]{3,2,1,0:T(8,128)(2,1)S(1)} async-done(((bf16[32,4,16,256]{3,2,1,0:T(8,128)(2,1)}), bf16[32,4,16,256]{3,2,1,0:T(8,128)(2,1)S(1)}, u32[]{:S(2)}, u32[]{:S(2)}) %all-to-all-start) | async-done | bytes 1048608 | tf_op jit(solution)/shard_map/all_to_all | solution.py:343
  33.8 4.3 %far.1 = bf16[32,4,16,256]{3,2,1,0:T(8,128)(2,1)} custom-call(bf16[32,4,16,256]{3,2,1,0:T(8,128)(2,1)S(1)} %all-to-all-done.arrived_ref, bf16[2,256,256]{2,1,0:T(8,128)(2,1)S(1)} %get-tuple-element.10.gather_ref, bf16[2,256,256]{2,1,0:T(8,128)(2,1)} %get-tuple-element.9.gather_hbm, bf16[1024,256]{1,0:T(8,128)(2,1)} %pad_maximum_fusion.spread_hbm, ...), custom_call_target="tpu_custom_call" | custom-call | tf_op jit(solution)/shard_map/far/pallas_call | solution.py:259
  38.1 4.6 %all-to-all-start.1 = ((bf16[32,4,16,256]{3,2,1,0:T(8,128)(2,1)}), bf16[32,4,16,256]{3,2,1,0:T(8,128)(2,1)S(1)}, u32[]{:S(2)}, u32[]{:S(2)}) async-start(bf16[32,4,16,256]{3,2,1,0:T(8,128)(2,1)} %far.1), calls=%async_computation.1 | async-start | bytes 2097152 | tf_op jit(solution)/shard_map/all_to_all | solution.py:343
  42.8 3.1 %collective-permute-start = (bf16[1,2,256,128]{3,2,1,0:T(8,128)(2,1)S(1)}, bf16[1,2,256,128]{3,2,1,0:T(8,128)(2,1)S(1)}, u32[]{:S(2)}, u32[]{:S(2)}) collective-permute-start(bf16[1,2,256,128]{3,2,1,0:T(8,128)(2,1)S(1)} %get-tuple-element.6), channel_id=1, source_target_pairs={{0,1},{1,2},{2,3},{3,4},{4,5},{5,6},{6,7},{7,8},{8,9},{9,10},{10,1... | collective-permute-start | bytes 393224 | tf_op jit(solution)/shard_map/ppermute | solution.py:329
  45.9 3.1 %collective-permute-start.1 = (bf16[1,2,256,128]{3,2,1,0:T(8,128)(2,1)S(1)}, bf16[1,2,256,128]{3,2,1,0:T(8,128)(2,1)S(1)}, u32[]{:S(2)}, u32[]{:S(2)}) collective-permute-start(bf16[1,2,256,128]{3,2,1,0:T(8,128)(2,1)S(1)} %get-tuple-element.5), channel_id=1, source_target_pairs={{1,0},{2,1},{3,2},{4,3},{5,4},{6,5},{7,6},{8,7},{9,8},{10,9},{11,1... | collective-permute-start | bytes 393224 | tf_op jit(solution)/shard_map/ppermute | solution.py:330
  49.0 21.1 %collective-permute-done.low_ref = bf16[1,2,256,128]{3,2,1,0:T(8,128)(2,1)S(1)} collective-permute-done((bf16[1,2,256,128]{3,2,1,0:T(8,128)(2,1)S(1)}, bf16[1,2,256,128]{3,2,1,0:T(8,128)(2,1)S(1)}, u32[]{:S(2)}, u32[]{:S(2)}) %collective-permute-start) | collective-permute-done | bytes 131104 | tf_op jit(solution)/shard_map/ppermute | solution.py:329
  70.1 0.7 copy-done.3
  70.8 2.8 %copy-done = bf16[8,3,2,256,256]{4,3,2,1,0:T(8,128)(2,1)S(1)} copy-done((bf16[8,3,2,256,256]{4,3,2,1,0:T(8,128)(2,1)S(1)}, bf16[8,3,2,256,256]{4,3,2,1,0:T(8,128)(2,1)}, u32[]{:S(2)}) %copy-start) | copy-done | bytes 6291480
  73.6 4.7 %near.1.near_ref = bf16[8,2,256,128]{3,2,1,0:T(8,128)(2,1)S(1)} custom-call(s32[1]{0:T(128)} %bitcast.place_ref, s32[2,256]{1,0:T(2,128)S(1)} %copy-done.2, bf16[8,2,256,128]{3,2,1,0:T(8,128)(2,1)S(1)} %copy-done.1, bf16[1,2,256,128]{3,2,1,0:T(8,128)(2,1)} %copy-done.3, bf16[1,2,256,128]{3,2,1,0:T(8,128)(2,1)} %copy-done.4, ...), custom_call_target="tpu_custom_call" | custom-call | tf_op jit(solution)/shard_map/near/pallas_call | solution.py:306
  78.3 1.6 %unpack.1 = bf16[8,2,256,128]{3,2,1,0:T(8,128)(2,1)} custom-call(bf16[8,2,256,128]{3,2,1,0:T(8,128)(2,1)S(1)} %near.1.near_ref, bf16[32,4,16,256]{3,2,1,0:T(8,128)(2,1)S(1)} %all-to-all-done.1.refs_0_), custom_call_target="tpu_custom_call" | custom-call | tf_op jit(solution)/shard_map/unpack/pallas_call | solution.py:168
  (22 shorter events, 0.4 us)
Async XLA Ops:
  2.8 31.1 %all-to-all-start = ((bf16[32,4,16,256]{3,2,1,0:T(8,128)(2,1)}), bf16[32,4,16,256]{3,2,1,0:T(8,128)(2,1)S(1)}, u32[]{:S(2)}, u32[]{:S(2)}) async-start(bf16[32,4,16,256]{3,2,1,0:T(8,128)(2,1)} %pack.1), calls=%async_computation | async-start | bytes 2097152 | tf_op jit(solution)/shard_map/all_to_all | solution.py:343
  11.3 31.5 %copy-start.1 = (bf16[8,2,256,128]{3,2,1,0:T(8,128)(2,1)S(1)}, bf16[8,2,256,128]{3,2,1,0:T(8,128)(2,1)}, u32[]{:S(2)}) copy-start(bf16[8,2,256,128]{3,2,1,0:T(8,128)(2,1)} %currents_ref.3) | copy-start | bytes 3145732
  12.6 58.2 %copy-start.2 = (s32[2,256]{1,0:T(2,128)S(1)}, s32[2,256]{1,0:T(2,128)}, u32[]{:S(2)}) copy-start(s32[2,256]{1,0:T(2,128)} %mask_ref.1) | copy-start | bytes 6148
  38.1 40.2 %all-to-all-start.1 = ((bf16[32,4,16,256]{3,2,1,0:T(8,128)(2,1)}), bf16[32,4,16,256]{3,2,1,0:T(8,128)(2,1)S(1)}, u32[]{:S(2)}, u32[]{:S(2)}) async-start(bf16[32,4,16,256]{3,2,1,0:T(8,128)(2,1)} %far.1), calls=%async_computation.1 | async-start | bytes 2097152 | tf_op jit(solution)/shard_map/all_to_all | solution.py:343
  42.8 27.3 %collective-permute-start = (bf16[1,2,256,128]{3,2,1,0:T(8,128)(2,1)S(1)}, bf16[1,2,256,128]{3,2,1,0:T(8,128)(2,1)S(1)}, u32[]{:S(2)}, u32[]{:S(2)}) collective-permute-start(bf16[1,2,256,128]{3,2,1,0:T(8,128)(2,1)S(1)} %get-tuple-element.6), channel_id=1, source_target_pairs={{0,1},{1,2},{2,3},{3,4},{4,5},{5,6},{6,7},{7,8},{8,9},{9,10},{10,1... | collective-permute-start | bytes 393224 | tf_op jit(solution)/shard_map/ppermute | solution.py:329
  45.9 24.2 %collective-permute-start.1 = (bf16[1,2,256,128]{3,2,1,0:T(8,128)(2,1)S(1)}, bf16[1,2,256,128]{3,2,1,0:T(8,128)(2,1)S(1)}, u32[]{:S(2)}, u32[]{:S(2)}) collective-permute-start(bf16[1,2,256,128]{3,2,1,0:T(8,128)(2,1)S(1)} %get-tuple-element.5), channel_id=1, source_target_pairs={{1,0},{2,1},{3,2},{4,3},{5,4},{6,5},{7,6},{8,7},{9,8},{10,9},{11,1... | collective-permute-start | bytes 393224 | tf_op jit(solution)/shard_map/ppermute | solution.py:330
  70.1 0.7 copy-start.3
  70.1 0.7 copy-start.4
  70.8 2.8 %copy-start = (bf16[8,3,2,256,256]{4,3,2,1,0:T(8,128)(2,1)S(1)}, bf16[8,3,2,256,256]{4,3,2,1,0:T(8,128)(2,1)}, u32[]{:S(2)}) copy-start(bf16[8,3,2,256,256]{4,3,2,1,0:T(8,128)(2,1)} %blocks_ref.1) | copy-start | bytes 18874372

commit v4 on v3

--- a/solution.py
+++ b/solution.py
@@ -6,14 +6,14 @@
 from jax import lax
 from jax.experimental import pallas as pl
 from jax.experimental.pallas import tpu as pltpu
-from jax.sharding import Mesh, PartitionSpec as P
+from jax.sharding import PartitionSpec as P
 
 
 wave_number = 2.0
 far_gain = 8.0
 golden_turn = 2.399963229728653
-axes = ("outer", "core", "far", "close")
-route = ("outer", "close", "core", "far")
+axes = ("box", "dir")
+route = ("dir", "box")
 chunks_wanted = 1
 far_rows = 512
 pack_waits = 4
@@ -276,33 +276,37 @@
     )(held(arrived), held(gather[:, :, :width]), far_away(later), far_away(spread), *[held(x) for x in (translate, cosine, sine)])
 
 
-def near_body(place_ref, mask_ref, currents_ref, low_ref, high_ref, blocks_ref, out_ref):
+def both_parts(block):
+    return jnp.concatenate([block[0], block[1]], 1)
+
+
+def joined(matrices, vectors):
+    angles = vectors[0].shape[1] // 2
+    by_re = by_im = 0.0
+    for matrix, vector in zip(matrices, vectors):
+        by_re += jnp.dot(matrix[0], vector, preferred_element_type=jnp.float32)
+        by_im += jnp.dot(matrix[1], vector, preferred_element_type=jnp.float32)
+    return by_re[:, :angles] - by_im[:, angles:], by_re[:, angles:] + by_im[:, :angles]
+
+
+def near_body(place_ref, mask_ref, currents_ref, blocks_ref, out_ref):
     boxes, _, unknowns, angles = currents_ref.shape
     box = pl.program_id(0)
     own = place_ref[0] * boxes + box
-
-    def both(block):
-        return jnp.concatenate([block[0], block[1]], 1)
-
     zero = jnp.zeros((unknowns, 2 * angles), jnp.bfloat16)
-    here = both(currents_ref[box])
-    before = jnp.where(box == 0, both(low_ref[0]), both(currents_ref[jnp.maximum(box - 1, 0)]))
-    after = jnp.where(
-        box == boxes - 1, both(high_ref[0]), both(currents_ref[jnp.minimum(box + 1, boxes - 1)])
+    here = both_parts(currents_ref[box])
+    before = both_parts(currents_ref[jnp.maximum(box - 1, 0)])
+    after = both_parts(currents_ref[jnp.minimum(box + 1, boxes - 1)])
+    before = jnp.where((mask_ref[0, own] == 1) & (box > 0), before, zero)
+    after = jnp.where((mask_ref[1, own] == 1) & (box < boxes - 1), after, zero)
+    blocks = blocks_ref[0]
+    out_ref[0, 0], out_ref[0, 1] = joined(
+        [blocks[0], blocks[1], blocks[2]], [here, before, after]
     )
-    before = jnp.where(mask_ref[0, own] == 1, before, zero)
-    after = jnp.where(mask_ref[1, own] == 1, after, zero)
-    by_re = jnp.zeros((unknowns, 2 * angles), jnp.float32)
-    by_im = jnp.zeros((unknowns, 2 * angles), jnp.float32)
-    for which, vectors in enumerate((here, before, after)):
-        by_re += jnp.dot(blocks_ref[0, which, 0], vectors, preferred_element_type=jnp.float32)
-        by_im += jnp.dot(blocks_ref[0, which, 1], vectors, preferred_element_type=jnp.float32)
-    out_ref[box, 0] = (by_re[:, :angles] - by_im[:, angles:]).astype(jnp.bfloat16)
-    out_ref[box, 1] = (by_re[:, angles:] + by_im[:, :angles]).astype(jnp.bfloat16)
-
-
-def near_field(currents, low, high, near_blocks, near_mask, place):
-    boxes, _, unknowns, _ = currents.shape
+
+
+def near_field(currents, near_blocks, near_mask, place):
+    boxes, _, unknowns, angles = currents.shape
     return pl.pallas_call(
         near_body,
         grid_spec=pltpu.PrefetchScalarGridSpec(
@@ -310,25 +314,72 @@
             grid=(boxes,),
             in_specs=[
                 vmem,
-                vmem,
-                vmem,
                 pl.BlockSpec((1, 3, 2, unknowns, unknowns), lambda i, *_: (i, 0, 0, 0, 0)),
             ],
-            out_specs=vmem,
+            out_specs=pl.BlockSpec((1, 2, unknowns, angles), lambda i, *_: (i, 0, 0, 0)),
         ),
-        out_shape=pltpu.VMEM(currents.shape, jnp.bfloat16),
+        out_shape=pltpu.HBM(currents.shape, jnp.float32),
         compiler_params=params,
         name="near",
-    )(place, near_mask, currents, low, high, near_blocks)
-
-
-def edges(currents):
+    )(place, near_mask, currents, near_blocks)
+
+
+def rim_body(place_ref, mask_ref, near_ref, one_ref, two_ref, blocks_hbm, out_ref, rim_ref, sems):
+    boxes, _, unknowns, angles = near_ref.shape
+    even = lax.rem(place_ref[0], 2) == 0
+    sides = ((0, 1), (boxes - 1, 2))
+    loads = [
+        pltpu.make_async_copy(blocks_hbm.at[box, which], rim_ref.at[which - 1], sems.at[which - 1])
+        for box, which in sides
+    ]
+    for load in loads:
+        load.start()
+    for box in range(1, boxes - 1):
+        out_ref[box] = near_ref[box].astype(jnp.bfloat16)
+    for load in loads:
+        load.wait()
+    zero = jnp.zeros((unknowns, 2 * angles), jnp.bfloat16)
+    totals = {}
+    one, two = both_parts(one_ref[0]), both_parts(two_ref[0])
+    edge = {1: jnp.where(even, two, one), 2: jnp.where(even, one, two)}
+    for box, which in sides:
+        on = mask_ref[which - 1, place_ref[0] * boxes + box] == 1
+        vectors = jnp.where(on, edge[which], zero)
+        more = joined([rim_ref[which - 1]], [vectors])
+        base = totals.get(box, (near_ref[box, 0], near_ref[box, 1]))
+        totals[box] = (base[0] + more[0], base[1] + more[1])
+    for box, total in totals.items():
+        out_ref[box, 0] = total[0].astype(jnp.bfloat16)
+        out_ref[box, 1] = total[1].astype(jnp.bfloat16)
+
+
+def with_rims(near, one, two, near_blocks, near_mask, place):
+    unknowns = near.shape[2]
+    scalars = pl.BlockSpec(memory_space=pltpu.SMEM)
+    return pl.pallas_call(
+        rim_body,
+        in_specs=[scalars, scalars, vmem, vmem, vmem, hbm],
+        out_specs=vmem,
+        out_shape=pltpu.VMEM(near.shape, jnp.bfloat16),
+        scratch_shapes=[
+            pltpu.VMEM((2, 2, unknowns, unknowns), jnp.bfloat16),
+            pltpu.SemaphoreType.DMA((2,)),
+        ],
+        compiler_params=params,
+        name="rim",
+    )(place, near_mask, near, one, two, far_away(near_blocks))
+
+
+def edges(currents, place):
     count = lax.axis_size(axes)
-    forward = [(i, i + 1) for i in range(count - 1)]
-    backward = [(i + 1, i) for i in range(count - 1)]
-    low = lax.ppermute(far_away(currents[-1:]), axes, forward)
-    high = lax.ppermute(far_away(currents[:1]), axes, backward)
-    return low, high
+    even = lax.rem(place[0], 2) == 0
+    first, last = currents[:1], currents[-1:]
+    above = [(i, i ^ 1) for i in range(count) if i ^ 1 < count]
+    below = [(i, i + 1) for i in range(1, count - 1, 2)]
+    below = below + [(target, source) for source, target in below]
+    one = lax.ppermute(far_away(jnp.where(even, last, first)), axes, above)
+    two = lax.ppermute(far_away(jnp.where(even, first, last)), axes, below)
+    return one, two
 
 
 def routed(values):
@@ -352,7 +403,7 @@
 
     packed = pack(currents, devices, chunks)
     arrived = [exchange(x) for x in packed]
-    low, high = edges(currents)
+    one, two = edges(currents, place)
     gather = aggregate.transpose(0, 2, 1)
     turned = disaggregate.transpose(0, 2, 1)
     spread = jnp.concatenate([turned[1], turned[0]], 0)
@@ -364,19 +415,15 @@
     sine = jnp.sin(theta)
     far = [far_field(x, gather, spread, translate, cosine, sine) for x in arrived]
     pieces = [exchange(x) for x in far]
-    near = near_field(currents, low, high, near_blocks, near_mask, place)
+    near = far_away(near_field(currents, near_blocks, near_mask, place))
+    near = with_rims(near, one, two, near_blocks, near_mask, place)
     return unpack(near, pieces, devices)
 
 
 def solution(mesh):
-    box, direction = (mesh.shape[axis] for axis in ("box", "dir"))
-    core = math.gcd(box, 2)
-    close = math.gcd(direction, 2)
-    shape = (box // core, core, direction // close, close)
-    finer = Mesh(mesh.devices.reshape(shape), axes)
     return jax.shard_map(
         product,
-        mesh=finer,
+        mesh=mesh,
         in_specs=(
             P(axes, None, None, None),
             P(axes, None, None, None, None),

time: 80.7 us -> 77.4 us (0.959)
  waiting for transfers between devices: 35.9 us -> 30.1 us
  Pallas kernels: 13.4 us -> 17.1 us
  starting transfers between devices: 17 us -> 15.5 us
    ppermute x2, waiting for transfers between devices: 21.1 us -> 15.2 us  [the longest x1 15.2 us: edges(): two = lax.ppermute(far_away(jnp.where(even, first, last)), axes, below)]
    pallas_call x0 -> x1, Pallas kernels: none -> 3.04 us  [with_rims(): pl.pallas_call(rim_body, in_specs=[scalars, scalars, vmem, vmem, vmem, hb...]
    ppermute x2, starting transfers between devices: 6.18 us -> 4.39 us  [the longest x1 3.09 us: edges(): two = lax.ppermute(far_away(jnp.where(even, first, last)), axes, below)]
  transfers between devices with their start and end apart: 4 -> 4, of which waited for: 2 -> 2; matrix products, arithmetic and copies ran while one was open for 12% -> 13% of each run, Pallas kernels for 6% -> 11%
where the time goes in v4:
time: 77.4 us; the launch traced here: 76.9 us
  waiting for transfers between devices  30.1 us (39%)
  Pallas kernels  17.1 us (22%)
  starting transfers between devices  15.5 us (20%)
  local copies, waits for them, and re-layouts  9.6 us (12%)
  other arithmetic  4.36 us (6%)
    ppermute x1, waiting for transfers between devices, edges(): two = lax.ppermute(far_away(jnp.where(even, first, last)), axes, below)  15.2 us
    all_to_all x2, waiting for transfers between devices, exchange(): return lax.all_to_all(value, route, split_axis=0, concat_axis=0, tiled=True)  15 us
    all_to_all x2, starting transfers between devices, exchange(): return lax.all_to_all(value, route, split_axis=0, concat_axis=0, tiled=True)  11.1 us
    unnamed x12, local copies, waits for them, and re-layouts  6.69 us
    pallas_call x1, Pallas kernels, near_field(): pl.pallas_call(near_body, grid_spec=pltpu.PrefetchScalarGridSpec(num_scal...  5.33 us
    pallas_call x1, Pallas kernels, far_field(): pl.pallas_call(far_body, in_specs=[vmem, vmem, hbm, hbm, vmem, vmem, vmem...  4.28 us
    ppermute x1, starting transfers between devices, edges(): two = lax.ppermute(far_away(jnp.where(even, first, last)), axes, below)  3.09 us
    pallas_call x1, Pallas kernels, with_rims(): pl.pallas_call(rim_body, in_specs=[scalars, scalars, vmem, vmem, vmem, hb...  3.04 us
  transfers between devices with their start and end apart: 4, of which 2 were waited for; matrix products, arithmetic and copies ran while one was open for 13% of the time, Pallas kernels for 11%

profile of v4, /device:TPU:17, one launch (start us, length us, event | category | flops | bytes accessed | tf_op | source)
XLA Modules:
  0.0 76.9 jit_solution(5652881296781622226)
XLA Ops:
  0.0 2.8 %pack.1 = bf16[32,4,16,256]{3,2,1,0:T(8,128)(2,1)} custom-call(bf16[8,2,256,128]{3,2,1,0:T(8,128)(2,1)} %currents_ref.3), custom_call_target="tpu_custom_call" | custom-call | tf_op jit(solution)/shard_map/pack/pallas_call | solution.py:117
  2.8 6.2 %all-to-all-start = ((bf16[32,4,16,256]{3,2,1,0:T(8,128)(2,1)}), bf16[32,4,16,256]{3,2,1,0:T(8,128)(2,1)S(1)}, u32[]{:S(2)}, u32[]{:S(2)}) async-start(bf16[32,4,16,256]{3,2,1,0:T(8,128)(2,1)} %pack.1), calls=%async_computation | async-start | bytes 2097152 | tf_op jit(solution)/shard_map/all_to_all | solution.py:394
  9.1 0.8 reshape.188
  10.0 0.1 eq.75
  10.1 0.8 %reshape.189 = f32[3,4,8,8]{3,2,1,0:T(8,128)S(1)} reshape(f32[3,256]{1,0:T(4,128)} %param.11) | data formatting | bytes 6144 | tf_op jit(solution)/shard_map/reshape | solution.py:387
  11.0 0.1 sub.86
  11.2 1.3 %copy.9 = bf16[2,512,256]{1,2,0:T(8,128)(2,1)S(1)} copy(bf16[2,512,256]{2,1,0:T(8,128)(2,1)} %param.9) | data formatting | bytes 1048576 | tf_op args[3]
  12.6 1.2 %copy.10 = bf16[2,256,512]{1,2,0:T(8,128)(2,1)S(1)} copy(bf16[2,256,512]{2,1,0:T(8,128)(2,1)} %param.10) | data formatting | bytes 1048576 | tf_op args[4]
  13.9 0.8 %pad_maximum_fusion.spread_hbm = bf16[1024,256]{1,0:T(8,128)(2,1)} fusion(bf16[512,256]{1,0:T(8,128)(2,1)S(1)} %get-tuple-element.8, bf16[512,256]{1,0:T(8,128)(2,1)S(1)} %get-tuple-element.7), kind=kLoop, calls=%fused_computation | loop fusion | flops 1048576 | bytes 1048576 | tf_op jit(solution)/shard_map/concatenate | solution.py:409
  14.8 1.4 %select_convert_fusion.translate_ref = bf16[256,256]{1,0:T(8,128)(2,1)S(1)} fusion(f32[256]{0:T(256)S(1)} %sub.86, f32[256]{0:T(256)S(1)} %sub.82, f32[256]{0:T(256)S(1)} %sub.78, s32[256]{0:T(256)S(1)} %reshape.187, s32[256]{0:T(256)S(1)} %get-tuple-element.19, s32[256]{0:T(256)S(1)} %get-tuple-element.18, pred[256]{0:T(512)(128)(4,1)S(1)} %eq.75, ...), kind=kLoop, calls=%fused_computation.6 | loop fusion | flops 1441792 | bytes 137728 | tf_op jit(solution)/shard_map/convert_element_type | solution.py:58
  16.2 0.7 fusion.2
  16.9 2.0 %fusion = (f32[256,512]{1,0:T(8,128)S(1)}, f32[256,512]{1,0:T(8,128)S(1)}) fusion(f32[512]{0:T(512)S(1)} %multiply_subtract_fusion, f32[256]{0:T(256)S(1)} %sub.86, f32[512]{0:T(512)S(1)} %get-tuple-element.20, f32[256]{0:T(256)S(1)} %sub.82, f32[512]{0:T(512)S(1)} %get-tuple-element.21, f32[256]{0:T(256)S(1)} %sub.78), kind=kLoop, calls=%fused_computation.2 | loop fusion | flops 786432 | bytes 1057792 | tf_op jit(solution)/shard_map/sin | solution.py:415
  19.0 15.0 %all-to-all-done.arrived_ref = bf16[32,4,16,256]{3,2,1,0:T(8,128)(2,1)S(1)} async-done(((bf16[32,4,16,256]{3,2,1,0:T(8,128)(2,1)}), bf16[32,4,16,256]{3,2,1,0:T(8,128)(2,1)S(1)}, u32[]{:S(2)}, u32[]{:S(2)}) %all-to-all-start) | async-done | bytes 1048608 | tf_op jit(solution)/shard_map/all_to_all | solution.py:394
  33.9 4.3 %far.1 = bf16[32,4,16,256]{3,2,1,0:T(8,128)(2,1)} custom-call(bf16[32,4,16,256]{3,2,1,0:T(8,128)(2,1)S(1)} %all-to-all-done.arrived_ref, bf16[2,256,256]{2,1,0:T(8,128)(2,1)S(1)} %get-tuple-element.10.gather_ref, bf16[2,256,256]{2,1,0:T(8,128)(2,1)} %get-tuple-element.9.gather_hbm, bf16[1024,256]{1,0:T(8,128)(2,1)} %pad_maximum_fusion.spread_hbm, ...), custom_call_target="tpu_custom_call" | custom-call | tf_op jit(solution)/shard_map/far/pallas_call | solution.py:259
  38.2 4.9 %all-to-all-start.1 = ((bf16[32,4,16,256]{3,2,1,0:T(8,128)(2,1)}), bf16[32,4,16,256]{3,2,1,0:T(8,128)(2,1)S(1)}, u32[]{:S(2)}, u32[]{:S(2)}) async-start(bf16[32,4,16,256]{3,2,1,0:T(8,128)(2,1)} %far.1), calls=%async_computation.1 | async-start | bytes 2097152 | tf_op jit(solution)/shard_map/all_to_all | solution.py:394
  43.2 3.1 %collective-permute-start.1 = (bf16[1,2,256,128]{3,2,1,0:T(8,128)(2,1)S(1)}, bf16[1,2,256,128]{3,2,1,0:T(8,128)(2,1)S(1)}, u32[]{:S(2)}, u32[]{:S(2)}) collective-permute-start(bf16[1,2,256,128]{3,2,1,0:T(8,128)(2,1)S(1)} %get-tuple-element.5), channel_id=1, source_target_pairs={{1,2},{3,4},{5,6},{7,8},{9,10},{11,12},{13,14},{15,16},{17,18},{19... | collective-permute-start | bytes 393224 | tf_op jit(solution)/shard_map/ppermute | solution.py:381
  46.3 1.3 %collective-permute-start = (bf16[1,2,256,128]{3,2,1,0:T(8,128)(2,1)S(1)}, bf16[1,2,256,128]{3,2,1,0:T(8,128)(2,1)S(1)}, u32[]{:S(2)}, u32[]{:S(2)}) collective-permute-start(bf16[1,2,256,128]{3,2,1,0:T(8,128)(2,1)S(1)} %get-tuple-element.6), channel_id=1, source_target_pairs={{0,1},{1,0},{2,3},{3,2},{4,5},{5,4},{6,7},{7,6},{8,9},{9,8},{10,11... | collective-permute-start | bytes 393224 | tf_op jit(solution)/shard_map/ppermute | solution.py:380
  47.6 2.8 %copy-done = bf16[8,3,2,256,256]{4,3,2,1,0:T(8,128)(2,1)S(1)} copy-done((bf16[8,3,2,256,256]{4,3,2,1,0:T(8,128)(2,1)S(1)}, bf16[8,3,2,256,256]{4,3,2,1,0:T(8,128)(2,1)}, u32[]{:S(2)}) %copy-start) | copy-done | bytes 6291480
  50.4 5.3 %near.1.near_ref = f32[8,2,256,128]{3,2,1,0:T(8,128)} custom-call(s32[1]{0:T(128)} %bitcast.place_ref, s32[2,256]{1,0:T(2,128)S(1)} %copy-done.2, bf16[8,2,256,128]{3,2,1,0:T(8,128)(2,1)S(1)} %copy-done.1, bf16[8,3,2,256,256]{4,3,2,1,0:T(8,128)(2,1)S(1)} %copy-done), custom_call_target="tpu_custom_call" | custom-call | tf_op jit(solution)/shard_map/near/pallas_call | solution.py:310
  55.7 15.2 %collective-permute-done.1.two_ref = bf16[1,2,256,128]{3,2,1,0:T(8,128)(2,1)S(1)} collective-permute-done((bf16[1,2,256,128]{3,2,1,0:T(8,128)(2,1)S(1)}, bf16[1,2,256,128]{3,2,1,0:T(8,128)(2,1)S(1)}, u32[]{:S(2)}, u32[]{:S(2)}) %collective-permute-start.1) | collective-permute-done | bytes 131104 | tf_op jit(solution)/shard_map/ppermute | solution.py:381
  70.9 0.6 copy-done.3
  71.5 0.7 copy-done.4
  72.2 3.0 %rim.1.near_ref = bf16[8,2,256,128]{3,2,1,0:T(8,128)(2,1)S(1)} custom-call(s32[1]{0:T(128)} %bitcast.place_ref, s32[2,256]{1,0:T(2,128)S(1)} %copy-done.2, f32[8,2,256,128]{3,2,1,0:T(8,128)} %near.1.near_ref, bf16[1,2,256,128]{3,2,1,0:T(8,128)(2,1)} %copy-done.4, bf16[1,2,256,128]{3,2,1,0:T(8,128)(2,1)} %copy-done.3, bf16[8,3,2,256,256]{4,3,2,1,0:T(8,128)(2,1)} %blocks_hbm.1), custom_call_target="tpu_custom_call" | custom-call | tf_op jit(solution)/shard_map/rim/pallas_call | solution.py:359
  75.2 1.6 %unpack.1 = bf16[8,2,256,128]{3,2,1,0:T(8,128)(2,1)} custom-call(bf16[8,2,256,128]{3,2,1,0:T(8,128)(2,1)S(1)} %rim.1.near_ref, bf16[32,4,16,256]{3,2,1,0:T(8,128)(2,1)S(1)} %all-to-all-done.1.refs_0_), custom_call_target="tpu_custom_call" | custom-call | tf_op jit(solution)/shard_map/unpack/pallas_call | solution.py:168
  (23 shorter events, 0.6 us)
Async XLA Ops:
  2.8 31.2 %all-to-all-start = ((bf16[32,4,16,256]{3,2,1,0:T(8,128)(2,1)}), bf16[32,4,16,256]{3,2,1,0:T(8,128)(2,1)S(1)}, u32[]{:S(2)}, u32[]{:S(2)}) async-start(bf16[32,4,16,256]{3,2,1,0:T(8,128)(2,1)} %pack.1), calls=%async_computation | async-start | bytes 2097152 | tf_op jit(solution)/shard_map/all_to_all | solution.py:394
  11.2 31.9 %copy-start.1 = (bf16[8,2,256,128]{3,2,1,0:T(8,128)(2,1)S(1)}, bf16[8,2,256,128]{3,2,1,0:T(8,128)(2,1)}, u32[]{:S(2)}) copy-start(bf16[8,2,256,128]{3,2,1,0:T(8,128)(2,1)} %currents_ref.3) | copy-start | bytes 3145732
  12.6 35.0 %copy-start.2 = (s32[2,256]{1,0:T(2,128)S(1)}, s32[2,256]{1,0:T(2,128)}, u32[]{:S(2)}) copy-start(s32[2,256]{1,0:T(2,128)} %mask_ref.3) | copy-start | bytes 6148
  38.2 37.0 %all-to-all-start.1 = ((bf16[32,4,16,256]{3,2,1,0:T(8,128)(2,1)}), bf16[32,4,16,256]{3,2,1,0:T(8,128)(2,1)S(1)}, u32[]{:S(2)}, u32[]{:S(2)}) async-start(bf16[32,4,16,256]{3,2,1,0:T(8,128)(2,1)} %far.1), calls=%async_computation.1 | async-start | bytes 2097152 | tf_op jit(solution)/shard_map/all_to_all | solution.py:394
  43.2 27.7 %collective-permute-start.1 = (bf16[1,2,256,128]{3,2,1,0:T(8,128)(2,1)S(1)}, bf16[1,2,256,128]{3,2,1,0:T(8,128)(2,1)S(1)}, u32[]{:S(2)}, u32[]{:S(2)}) collective-permute-start(bf16[1,2,256,128]{3,2,1,0:T(8,128)(2,1)S(1)} %get-tuple-element.5), channel_id=1, source_target_pairs={{1,2},{3,4},{5,6},{7,8},{9,10},{11,12},{13,14},{15,16},{17,18},{19... | collective-permute-start | bytes 393224 | tf_op jit(solution)/shard_map/ppermute | solution.py:381
  46.3 24.6 %collective-permute-start = (bf16[1,2,256,128]{3,2,1,0:T(8,128)(2,1)S(1)}, bf16[1,2,256,128]{3,2,1,0:T(8,128)(2,1)S(1)}, u32[]{:S(2)}, u32[]{:S(2)}) collective-permute-start(bf16[1,2,256,128]{3,2,1,0:T(8,128)(2,1)S(1)} %get-tuple-element.6), channel_id=1, source_target_pairs={{0,1},{1,0},{2,3},{3,2},{4,5},{5,4},{6,7},{7,6},{8,9},{9,8},{10,11... | collective-permute-start | bytes 393224 | tf_op jit(solution)/shard_map/ppermute | solution.py:380
  47.6 2.8 %copy-start = (bf16[8,3,2,256,256]{4,3,2,1,0:T(8,128)(2,1)S(1)}, bf16[8,3,2,256,256]{4,3,2,1,0:T(8,128)(2,1)}, u32[]{:S(2)}) copy-start(bf16[8,3,2,256,256]{4,3,2,1,0:T(8,128)(2,1)} %blocks_hbm.1) | copy-start | bytes 18874372
  70.9 0.7 copy-start.3
  71.5 0.7 copy-start.4

commit v5 on v4

--- a/solution.py
+++ b/solution.py
@@ -15,8 +15,9 @@
 axes = ("box", "dir")
 route = ("dir", "box")
 chunks_wanted = 1
-far_rows = 512
-pack_waits = 4
+packed = pltpu.CompilerParams(vmem_limit_bytes=20 << 20)
+far_rows = 1024
+pack_waits = 2
 far_slots = 1
 hbm = pl.BlockSpec(memory_space=pltpu.HBM)
 vmem = pl.BlockSpec(memory_space=pltpu.VMEM)
@@ -175,7 +176,7 @@
             pltpu.VMEM(near.shape, jnp.bfloat16),
             pltpu.SemaphoreType.DMA((boxes,)),
         ],
-        compiler_params=params,
+        compiler_params=packed,
         name="unpack",
     )(held(near), *[held(x) for x in pieces])
 

time: 77.4 us -> 77.4 us (level)
  no operation moved by 1% of the time
where the time goes in v5:
time: 77.4 us; the launch traced here: 76.9 us
  waiting for transfers between devices  30.1 us (39%)
  Pallas kernels  17 us (22%)
  starting transfers between devices  15.5 us (20%)
  local copies, waits for them, and re-layouts  9.6 us (12%)
  other arithmetic  4.36 us (6%)
    ppermute x1, waiting for transfers between devices, edges(): two = lax.ppermute(far_away(jnp.where(even, first, last)), axes, below)  15.2 us
    all_to_all x2, waiting for transfers between devices, exchange(): return lax.all_to_all(value, route, split_axis=0, concat_axis=0, tiled=True)  15 us
    all_to_all x2, starting transfers between devices, exchange(): return lax.all_to_all(value, route, split_axis=0, concat_axis=0, tiled=True)  11.1 us
    unnamed x12, local copies, waits for them, and re-layouts  6.69 us
    pallas_call x1, Pallas kernels, near_field(): pl.pallas_call(near_body, grid_spec=pltpu.PrefetchScalarGridSpec(num_scal...  5.33 us
    pallas_call x1, Pallas kernels, far_field(): pl.pallas_call(far_body, in_specs=[vmem, vmem, hbm, hbm, vmem, vmem, vmem...  4.28 us
    ppermute x1, starting transfers between devices, edges(): two = lax.ppermute(far_away(jnp.where(even, first, last)), axes, below)  3.09 us
    pallas_call x1, Pallas kernels, with_rims(): pl.pallas_call(rim_body, in_specs=[scalars, scalars, vmem, vmem, vmem, hb...  3.04 us
  transfers between devices with their start and end apart: 4, of which 2 were waited for; matrix products, arithmetic and copies ran while one was open for 13% of the time, Pallas kernels for 11%

profile of v5, /device:TPU:17, one launch (start us, length us, event | category | flops | bytes accessed | tf_op | source)
XLA Modules:
  0.0 76.9 jit_solution(18411093054615404235)
XLA Ops:
  0.0 2.8 %pack.1 = bf16[32,4,16,256]{3,2,1,0:T(8,128)(2,1)} custom-call(bf16[8,2,256,128]{3,2,1,0:T(8,128)(2,1)} %currents_ref.3), custom_call_target="tpu_custom_call" | custom-call | tf_op jit(solution)/shard_map/pack/pallas_call | solution.py:118
  2.8 6.2 %all-to-all-start = ((bf16[32,4,16,256]{3,2,1,0:T(8,128)(2,1)}), bf16[32,4,16,256]{3,2,1,0:T(8,128)(2,1)S(1)}, u32[]{:S(2)}, u32[]{:S(2)}) async-start(bf16[32,4,16,256]{3,2,1,0:T(8,128)(2,1)} %pack.1), calls=%async_computation | async-start | bytes 2097152 | tf_op jit(solution)/shard_map/all_to_all | solution.py:395
  9.1 0.8 reshape.188
  10.0 0.1 eq.75
  10.1 0.8 %reshape.189 = f32[3,4,8,8]{3,2,1,0:T(8,128)S(1)} reshape(f32[3,256]{1,0:T(4,128)} %param.11) | data formatting | bytes 6144 | tf_op jit(solution)/shard_map/reshape | solution.py:388
  11.1 0.1 sub.82
  11.2 1.3 %copy.9 = bf16[2,512,256]{1,2,0:T(8,128)(2,1)S(1)} copy(bf16[2,512,256]{2,1,0:T(8,128)(2,1)} %param.9) | data formatting | bytes 1048576 | tf_op args[3]
  12.6 1.2 %copy.10 = bf16[2,256,512]{1,2,0:T(8,128)(2,1)S(1)} copy(bf16[2,256,512]{2,1,0:T(8,128)(2,1)} %param.10) | data formatting | bytes 1048576 | tf_op args[4]
  13.9 0.8 %pad_maximum_fusion.spread_hbm = bf16[1024,256]{1,0:T(8,128)(2,1)} fusion(bf16[512,256]{1,0:T(8,128)(2,1)S(1)} %get-tuple-element.8, bf16[512,256]{1,0:T(8,128)(2,1)S(1)} %get-tuple-element.7), kind=kLoop, calls=%fused_computation | loop fusion | flops 1048576 | bytes 1048576 | tf_op jit(solution)/shard_map/concatenate | solution.py:410
  14.8 1.4 %select_convert_fusion.translate_ref = bf16[256,256]{1,0:T(8,128)(2,1)S(1)} fusion(f32[256]{0:T(256)S(1)} %sub.86, f32[256]{0:T(256)S(1)} %sub.82, f32[256]{0:T(256)S(1)} %sub.78, s32[256]{0:T(256)S(1)} %reshape.187, s32[256]{0:T(256)S(1)} %get-tuple-element.19, s32[256]{0:T(256)S(1)} %get-tuple-element.18, pred[256]{0:T(512)(128)(4,1)S(1)} %eq.75, ...), kind=kLoop, calls=%fused_computation.6 | loop fusion | flops 1441792 | bytes 137728 | tf_op jit(solution)/shard_map/convert_element_type | solution.py:59
  16.2 0.7 fusion.2
  16.9 2.0 %fusion = (f32[256,512]{1,0:T(8,128)S(1)}, f32[256,512]{1,0:T(8,128)S(1)}) fusion(f32[512]{0:T(512)S(1)} %multiply_subtract_fusion, f32[256]{0:T(256)S(1)} %sub.86, f32[512]{0:T(512)S(1)} %get-tuple-element.20, f32[256]{0:T(256)S(1)} %sub.82, f32[512]{0:T(512)S(1)} %get-tuple-element.21, f32[256]{0:T(256)S(1)} %sub.78), kind=kLoop, calls=%fused_computation.2 | loop fusion | flops 786432 | bytes 1057792 | tf_op jit(solution)/shard_map/sin | solution.py:416
  18.9 15.0 %all-to-all-done.arrived_ref = bf16[32,4,16,256]{3,2,1,0:T(8,128)(2,1)S(1)} async-done(((bf16[32,4,16,256]{3,2,1,0:T(8,128)(2,1)}), bf16[32,4,16,256]{3,2,1,0:T(8,128)(2,1)S(1)}, u32[]{:S(2)}, u32[]{:S(2)}) %all-to-all-start) | async-done | bytes 1048608 | tf_op jit(solution)/shard_map/all_to_all | solution.py:395
  33.9 4.3 %far.1 = bf16[32,4,16,256]{3,2,1,0:T(8,128)(2,1)} custom-call(bf16[32,4,16,256]{3,2,1,0:T(8,128)(2,1)S(1)} %all-to-all-done.arrived_ref, bf16[2,256,256]{2,1,0:T(8,128)(2,1)S(1)} %get-tuple-element.10.gather_ref, bf16[2,256,256]{2,1,0:T(8,128)(2,1)} %get-tuple-element.9.gather_hbm, bf16[1024,256]{1,0:T(8,128)(2,1)} %pad_maximum_fusion.spread_hbm, ...), custom_call_target="tpu_custom_call" | custom-call | tf_op jit(solution)/shard_map/far/pallas_call | solution.py:260
  38.2 4.9 %all-to-all-start.1 = ((bf16[32,4,16,256]{3,2,1,0:T(8,128)(2,1)}), bf16[32,4,16,256]{3,2,1,0:T(8,128)(2,1)S(1)}, u32[]{:S(2)}, u32[]{:S(2)}) async-start(bf16[32,4,16,256]{3,2,1,0:T(8,128)(2,1)} %far.1), calls=%async_computation.1 | async-start | bytes 2097152 | tf_op jit(solution)/shard_map/all_to_all | solution.py:395
  43.2 3.1 %collective-permute-start.1 = (bf16[1,2,256,128]{3,2,1,0:T(8,128)(2,1)S(1)}, bf16[1,2,256,128]{3,2,1,0:T(8,128)(2,1)S(1)}, u32[]{:S(2)}, u32[]{:S(2)}) collective-permute-start(bf16[1,2,256,128]{3,2,1,0:T(8,128)(2,1)S(1)} %get-tuple-element.5), channel_id=1, source_target_pairs={{1,2},{3,4},{5,6},{7,8},{9,10},{11,12},{13,14},{15,16},{17,18},{19... | collective-permute-start | bytes 393224 | tf_op jit(solution)/shard_map/ppermute | solution.py:382
  46.2 1.3 %collective-permute-start = (bf16[1,2,256,128]{3,2,1,0:T(8,128)(2,1)S(1)}, bf16[1,2,256,128]{3,2,1,0:T(8,128)(2,1)S(1)}, u32[]{:S(2)}, u32[]{:S(2)}) collective-permute-start(bf16[1,2,256,128]{3,2,1,0:T(8,128)(2,1)S(1)} %get-tuple-element.6), channel_id=1, source_target_pairs={{0,1},{1,0},{2,3},{3,2},{4,5},{5,4},{6,7},{7,6},{8,9},{9,8},{10,11... | collective-permute-start | bytes 393224 | tf_op jit(solution)/shard_map/ppermute | solution.py:381
  47.6 2.8 %copy-done = bf16[8,3,2,256,256]{4,3,2,1,0:T(8,128)(2,1)S(1)} copy-done((bf16[8,3,2,256,256]{4,3,2,1,0:T(8,128)(2,1)S(1)}, bf16[8,3,2,256,256]{4,3,2,1,0:T(8,128)(2,1)}, u32[]{:S(2)}) %copy-start) | copy-done | bytes 6291480
  50.3 5.3 %near.1.near_ref = f32[8,2,256,128]{3,2,1,0:T(8,128)} custom-call(s32[1]{0:T(128)} %bitcast.place_ref, s32[2,256]{1,0:T(2,128)S(1)} %copy-done.2, bf16[8,2,256,128]{3,2,1,0:T(8,128)(2,1)S(1)} %copy-done.1, bf16[8,3,2,256,256]{4,3,2,1,0:T(8,128)(2,1)S(1)} %copy-done), custom_call_target="tpu_custom_call" | custom-call | tf_op jit(solution)/shard_map/near/pallas_call | solution.py:311
  55.7 15.2 %collective-permute-done.1.two_ref = bf16[1,2,256,128]{3,2,1,0:T(8,128)(2,1)S(1)} collective-permute-done((bf16[1,2,256,128]{3,2,1,0:T(8,128)(2,1)S(1)}, bf16[1,2,256,128]{3,2,1,0:T(8,128)(2,1)S(1)}, u32[]{:S(2)}, u32[]{:S(2)}) %collective-permute-start.1) | collective-permute-done | bytes 131104 | tf_op jit(solution)/shard_map/ppermute | solution.py:382
  70.8 0.6 copy-done.3
  71.5 0.7 copy-done.4
  72.1 3.0 %rim.1.near_ref = bf16[8,2,256,128]{3,2,1,0:T(8,128)(2,1)S(1)} custom-call(s32[1]{0:T(128)} %bitcast.place_ref, s32[2,256]{1,0:T(2,128)S(1)} %copy-done.2, f32[8,2,256,128]{3,2,1,0:T(8,128)} %near.1.near_ref, bf16[1,2,256,128]{3,2,1,0:T(8,128)(2,1)} %copy-done.4, bf16[1,2,256,128]{3,2,1,0:T(8,128)(2,1)} %copy-done.3, bf16[8,3,2,256,256]{4,3,2,1,0:T(8,128)(2,1)} %blocks_hbm.1), custom_call_target="tpu_custom_call" | custom-call | tf_op jit(solution)/shard_map/rim/pallas_call | solution.py:360
  75.2 1.6 %unpack.1 = bf16[8,2,256,128]{3,2,1,0:T(8,128)(2,1)} custom-call(bf16[8,2,256,128]{3,2,1,0:T(8,128)(2,1)S(1)} %rim.1.near_ref, bf16[32,4,16,256]{3,2,1,0:T(8,128)(2,1)S(1)} %all-to-all-done.1.refs_0_), custom_call_target="tpu_custom_call" | custom-call | tf_op jit(solution)/shard_map/unpack/pallas_call | solution.py:169
  (23 shorter events, 0.6 us)
Async XLA Ops:
  2.8 31.2 %all-to-all-start = ((bf16[32,4,16,256]{3,2,1,0:T(8,128)(2,1)}), bf16[32,4,16,256]{3,2,1,0:T(8,128)(2,1)S(1)}, u32[]{:S(2)}, u32[]{:S(2)}) async-start(bf16[32,4,16,256]{3,2,1,0:T(8,128)(2,1)} %pack.1), calls=%async_computation | async-start | bytes 2097152 | tf_op jit(solution)/shard_map/all_to_all | solution.py:395
  11.2 31.9 %copy-start.1 = (bf16[8,2,256,128]{3,2,1,0:T(8,128)(2,1)S(1)}, bf16[8,2,256,128]{3,2,1,0:T(8,128)(2,1)}, u32[]{:S(2)}) copy-start(bf16[8,2,256,128]{3,2,1,0:T(8,128)(2,1)} %currents_ref.3) | copy-start | bytes 3145732
  12.6 35.0 %copy-start.2 = (s32[2,256]{1,0:T(2,128)S(1)}, s32[2,256]{1,0:T(2,128)}, u32[]{:S(2)}) copy-start(s32[2,256]{1,0:T(2,128)} %mask_ref.3) | copy-start | bytes 6148
  38.2 37.0 %all-to-all-start.1 = ((bf16[32,4,16,256]{3,2,1,0:T(8,128)(2,1)}), bf16[32,4,16,256]{3,2,1,0:T(8,128)(2,1)S(1)}, u32[]{:S(2)}, u32[]{:S(2)}) async-start(bf16[32,4,16,256]{3,2,1,0:T(8,128)(2,1)} %far.1), calls=%async_computation.1 | async-start | bytes 2097152 | tf_op jit(solution)/shard_map/all_to_all | solution.py:395
  43.2 27.7 %collective-permute-start.1 = (bf16[1,2,256,128]{3,2,1,0:T(8,128)(2,1)S(1)}, bf16[1,2,256,128]{3,2,1,0:T(8,128)(2,1)S(1)}, u32[]{:S(2)}, u32[]{:S(2)}) collective-permute-start(bf16[1,2,256,128]{3,2,1,0:T(8,128)(2,1)S(1)} %get-tuple-element.5), channel_id=1, source_target_pairs={{1,2},{3,4},{5,6},{7,8},{9,10},{11,12},{13,14},{15,16},{17,18},{19... | collective-permute-start | bytes 393224 | tf_op jit(solution)/shard_map/ppermute | solution.py:382
  46.2 24.6 %collective-permute-start = (bf16[1,2,256,128]{3,2,1,0:T(8,128)(2,1)S(1)}, bf16[1,2,256,128]{3,2,1,0:T(8,128)(2,1)S(1)}, u32[]{:S(2)}, u32[]{:S(2)}) collective-permute-start(bf16[1,2,256,128]{3,2,1,0:T(8,128)(2,1)S(1)} %get-tuple-element.6), channel_id=1, source_target_pairs={{0,1},{1,0},{2,3},{3,2},{4,5},{5,4},{6,7},{7,6},{8,9},{9,8},{10,11... | collective-permute-start | bytes 393224 | tf_op jit(solution)/shard_map/ppermute | solution.py:381
  47.6 2.8 %copy-start = (bf16[8,3,2,256,256]{4,3,2,1,0:T(8,128)(2,1)S(1)}, bf16[8,3,2,256,256]{4,3,2,1,0:T(8,128)(2,1)}, u32[]{:S(2)}) copy-start(bf16[8,3,2,256,256]{4,3,2,1,0:T(8,128)(2,1)} %blocks_hbm.1) | copy-start | bytes 18874372
  70.8 0.7 copy-start.3
  71.5 0.7 copy-start.4

commit v6 on v5

--- a/solution.py
+++ b/solution.py
@@ -3,6 +3,7 @@
 
 import jax
 import jax.numpy as jnp
+import numpy as np
 from jax import lax
 from jax.experimental import pallas as pl
 from jax.experimental.pallas import tpu as pltpu
@@ -17,7 +18,7 @@
 chunks_wanted = 1
 packed = pltpu.CompilerParams(vmem_limit_bytes=20 << 20)
 far_rows = 1024
-pack_waits = 2
+pack_waits = 4
 far_slots = 1
 hbm = pl.BlockSpec(memory_space=pltpu.HBM)
 vmem = pl.BlockSpec(memory_space=pltpu.VMEM)
@@ -65,6 +66,12 @@
     col = lax.broadcasted_iota(jnp.int32, (size, size), 1)
     source = lax.rem(row, inner) * outer + lax.div(row, inner)
     return jnp.where(source == col, 1.0, 0.0).astype(jnp.bfloat16)
+
+
+def swap_table(outer, inner):
+    row = np.arange(outer * inner)
+    source = (row % inner) * outer + row // inner
+    return jnp.asarray(source[:, None] == row[None, :], jnp.bfloat16)
 
 
 def held(value):
@@ -132,12 +139,12 @@
     )(far_away(currents))
 
 
-def unpack_body(near_ref, *refs, devices, angles_each, group):
+def unpack_body(near_ref, swap_ref, *refs, devices, angles_each, group):
     ins, (out_ref, turned_ref, done_ref, sems) = refs[:-4], refs[-4:]
     boxes, _, unknowns, angles = near_ref.shape
     rows = 2 * boxes
     per_in = angles_each // len(ins)
-    swap = swap_matrix(rows, group)
+    swap = swap_ref[...]
     for first in range(0, angles, group):
         own, device = divmod(first, devices)
         which, slot = divmod(own, per_in)
@@ -168,7 +175,7 @@
     body = functools.partial(unpack_body, devices=devices, angles_each=angles_each, group=group)
     return pl.pallas_call(
         body,
-        in_specs=[vmem] * (1 + len(pieces)),
+        in_specs=[vmem] * (2 + len(pieces)),
         out_specs=hbm,
         out_shape=jax.ShapeDtypeStruct(near.shape, jnp.bfloat16),
         scratch_shapes=[
@@ -178,7 +185,7 @@
         ],
         compiler_params=packed,
         name="unpack",
-    )(held(near), *[held(x) for x in pieces])
+    )(held(near), held(swap_table(rows, group)), *[held(x) for x in pieces])
 
 
 def far_body(

time: 77.4 us -> 77.4 us (level)
    unnamed x12 -> x14, local copies, waits for them, and re-layouts: 6.69 us -> 6.67 us
where the time goes in v6:
time: 77.4 us; the launch traced here: 76.9 us
  waiting for transfers between devices  30.2 us (39%)
  Pallas kernels  17.1 us (22%)
  starting transfers between devices  15.5 us (20%)
  local copies, waits for them, and re-layouts  9.57 us (12%)
  other arithmetic  4.35 us (6%)
    ppermute x1, waiting for transfers between devices, edges(): two = lax.ppermute(far_away(jnp.where(even, first, last)), axes, below)  15.2 us
    all_to_all x2, waiting for transfers between devices, exchange(): return lax.all_to_all(value, route, split_axis=0, concat_axis=0, tiled=True)  15 us
    all_to_all x2, starting transfers between devices, exchange(): return lax.all_to_all(value, route, split_axis=0, concat_axis=0, tiled=True)  11.1 us
    unnamed x14, local copies, waits for them, and re-layouts  6.67 us
    pallas_call x1, Pallas kernels, near_field(): pl.pallas_call(near_body, grid_spec=pltpu.PrefetchScalarGridSpec(num_scal...  5.32 us
    pallas_call x1, Pallas kernels, far_field(): pl.pallas_call(far_body, in_specs=[vmem, vmem, hbm, hbm, vmem, vmem, vmem...  4.28 us
    ppermute x1, starting transfers between devices, edges(): two = lax.ppermute(far_away(jnp.where(even, first, last)), axes, below)  3.09 us
    pallas_call x1, Pallas kernels, with_rims(): pl.pallas_call(rim_body, in_specs=[scalars, scalars, vmem, vmem, vmem, hb...  3.04 us
  transfers between devices with their start and end apart: 4, of which 2 were waited for; matrix products, arithmetic and copies ran while one was open for 13% of the time, Pallas kernels for 11%

profile of v6, /device:TPU:17, one launch (start us, length us, event | category | flops | bytes accessed | tf_op | source)
XLA Modules:
  0.0 76.9 jit_solution(12906073839070523364)
XLA Ops:
  0.0 2.8 %pack.1 = bf16[32,4,16,256]{3,2,1,0:T(8,128)(2,1)} custom-call(bf16[8,2,256,128]{3,2,1,0:T(8,128)(2,1)} %currents_ref.3), custom_call_target="tpu_custom_call" | custom-call | tf_op jit(solution)/shard_map/pack/pallas_call | solution.py:125
  2.8 6.2 %all-to-all-start = ((bf16[32,4,16,256]{3,2,1,0:T(8,128)(2,1)}), bf16[32,4,16,256]{3,2,1,0:T(8,128)(2,1)S(1)}, u32[]{:S(2)}, u32[]{:S(2)}) async-start(bf16[32,4,16,256]{3,2,1,0:T(8,128)(2,1)} %pack.1), calls=%async_computation | async-start | bytes 2097152 | tf_op jit(solution)/shard_map/all_to_all | solution.py:402
  9.1 0.8 reshape.188
  10.0 0.1 eq.75
  10.1 0.8 %reshape.189 = f32[3,4,8,8]{3,2,1,0:T(8,128)S(1)} reshape(f32[3,256]{1,0:T(4,128)} %param.12) | data formatting | bytes 6144 | tf_op jit(solution)/shard_map/reshape | solution.py:395
  11.0 0.1 sub.86
  11.2 1.3 %copy.10 = bf16[2,512,256]{1,2,0:T(8,128)(2,1)S(1)} copy(bf16[2,512,256]{2,1,0:T(8,128)(2,1)} %param.10) | data formatting | bytes 1048576 | tf_op args[3]
  12.6 1.2 %copy.11 = bf16[2,256,512]{1,2,0:T(8,128)(2,1)S(1)} copy(bf16[2,256,512]{2,1,0:T(8,128)(2,1)} %param.11) | data formatting | bytes 1048576 | tf_op args[4]
  13.9 0.8 %pad_maximum_fusion.spread_hbm = bf16[1024,256]{1,0:T(8,128)(2,1)} fusion(bf16[512,256]{1,0:T(8,128)(2,1)S(1)} %get-tuple-element.8, bf16[512,256]{1,0:T(8,128)(2,1)S(1)} %get-tuple-element.7), kind=kLoop, calls=%fused_computation | loop fusion | flops 1048576 | bytes 1048576 | tf_op jit(solution)/shard_map/concatenate | solution.py:417
  14.8 1.4 %select_convert_fusion.translate_ref = bf16[256,256]{1,0:T(8,128)(2,1)S(1)} fusion(f32[256]{0:T(256)S(1)} %sub.86, f32[256]{0:T(256)S(1)} %sub.82, f32[256]{0:T(256)S(1)} %sub.78, s32[256]{0:T(256)S(1)} %reshape.187, s32[256]{0:T(256)S(1)} %get-tuple-element.19, s32[256]{0:T(256)S(1)} %get-tuple-element.18, pred[256]{0:T(512)(128)(4,1)S(1)} %eq.75, ...), kind=kLoop, calls=%fused_computation.6 | loop fusion | flops 1441792 | bytes 137728 | tf_op jit(solution)/shard_map/convert_element_type | solution.py:60
  16.2 0.7 fusion.2
  16.9 2.0 %fusion = (f32[256,512]{1,0:T(8,128)S(1)}, f32[256,512]{1,0:T(8,128)S(1)}) fusion(f32[512]{0:T(512)S(1)} %multiply_subtract_fusion, f32[256]{0:T(256)S(1)} %sub.86, f32[512]{0:T(512)S(1)} %get-tuple-element.20, f32[256]{0:T(256)S(1)} %sub.82, f32[512]{0:T(512)S(1)} %get-tuple-element.21, f32[256]{0:T(256)S(1)} %sub.78), kind=kLoop, calls=%fused_computation.2 | loop fusion | flops 786432 | bytes 1057792 | tf_op jit(solution)/shard_map/sin | solution.py:423
  19.0 15.0 %all-to-all-done.arrived_ref = bf16[32,4,16,256]{3,2,1,0:T(8,128)(2,1)S(1)} async-done(((bf16[32,4,16,256]{3,2,1,0:T(8,128)(2,1)}), bf16[32,4,16,256]{3,2,1,0:T(8,128)(2,1)S(1)}, u32[]{:S(2)}, u32[]{:S(2)}) %all-to-all-start) | async-done | bytes 1048608 | tf_op jit(solution)/shard_map/all_to_all | solution.py:402
  33.9 4.3 %far.1 = bf16[32,4,16,256]{3,2,1,0:T(8,128)(2,1)} custom-call(bf16[32,4,16,256]{3,2,1,0:T(8,128)(2,1)S(1)} %all-to-all-done.arrived_ref, bf16[2,256,256]{2,1,0:T(8,128)(2,1)S(1)} %get-tuple-element.10.gather_ref, bf16[2,256,256]{2,1,0:T(8,128)(2,1)} %get-tuple-element.9.gather_hbm, bf16[1024,256]{1,0:T(8,128)(2,1)} %pad_maximum_fusion.spread_hbm, ...), custom_call_target="tpu_custom_call" | custom-call | tf_op jit(solution)/shard_map/far/pallas_call | solution.py:267
  38.2 4.9 %all-to-all-start.1 = ((bf16[32,4,16,256]{3,2,1,0:T(8,128)(2,1)}), bf16[32,4,16,256]{3,2,1,0:T(8,128)(2,1)S(1)}, u32[]{:S(2)}, u32[]{:S(2)}) async-start(bf16[32,4,16,256]{3,2,1,0:T(8,128)(2,1)} %far.1), calls=%async_computation.1 | async-start | bytes 2097152 | tf_op jit(solution)/shard_map/all_to_all | solution.py:402
  43.2 3.1 %collective-permute-start.1 = (bf16[1,2,256,128]{3,2,1,0:T(8,128)(2,1)S(1)}, bf16[1,2,256,128]{3,2,1,0:T(8,128)(2,1)S(1)}, u32[]{:S(2)}, u32[]{:S(2)}) collective-permute-start(bf16[1,2,256,128]{3,2,1,0:T(8,128)(2,1)S(1)} %get-tuple-element.5), channel_id=1, source_target_pairs={{1,2},{3,4},{5,6},{7,8},{9,10},{11,12},{13,14},{15,16},{17,18},{19... | collective-permute-start | bytes 393224 | tf_op jit(solution)/shard_map/ppermute | solution.py:389
  46.3 1.3 %collective-permute-start = (bf16[1,2,256,128]{3,2,1,0:T(8,128)(2,1)S(1)}, bf16[1,2,256,128]{3,2,1,0:T(8,128)(2,1)S(1)}, u32[]{:S(2)}, u32[]{:S(2)}) collective-permute-start(bf16[1,2,256,128]{3,2,1,0:T(8,128)(2,1)S(1)} %get-tuple-element.6), channel_id=1, source_target_pairs={{0,1},{1,0},{2,3},{3,2},{4,5},{5,4},{6,7},{7,6},{8,9},{9,8},{10,11... | collective-permute-start | bytes 393224 | tf_op jit(solution)/shard_map/ppermute | solution.py:388
  47.6 2.8 %copy-done = bf16[8,3,2,256,256]{4,3,2,1,0:T(8,128)(2,1)S(1)} copy-done((bf16[8,3,2,256,256]{4,3,2,1,0:T(8,128)(2,1)S(1)}, bf16[8,3,2,256,256]{4,3,2,1,0:T(8,128)(2,1)}, u32[]{:S(2)}) %copy-start) | copy-done | bytes 6291480
  50.4 5.3 %near.1.near_ref = f32[8,2,256,128]{3,2,1,0:T(8,128)} custom-call(s32[1]{0:T(128)} %bitcast.place_ref, s32[2,256]{1,0:T(2,128)S(1)} %copy-done.3, bf16[8,2,256,128]{3,2,1,0:T(8,128)(2,1)S(1)} %copy-done.1, bf16[8,3,2,256,256]{4,3,2,1,0:T(8,128)(2,1)S(1)} %copy-done), custom_call_target="tpu_custom_call" | custom-call | tf_op jit(solution)/shard_map/near/pallas_call | solution.py:318
  55.7 15.2 %collective-permute-done.1.two_ref = bf16[1,2,256,128]{3,2,1,0:T(8,128)(2,1)S(1)} collective-permute-done((bf16[1,2,256,128]{3,2,1,0:T(8,128)(2,1)S(1)}, bf16[1,2,256,128]{3,2,1,0:T(8,128)(2,1)S(1)}, u32[]{:S(2)}, u32[]{:S(2)}) %collective-permute-start.1) | collective-permute-done | bytes 131104 | tf_op jit(solution)/shard_map/ppermute | solution.py:389
  70.9 0.6 copy-done.4
  71.5 0.6 copy-done.5
  72.1 3.0 %rim.1.near_ref = bf16[8,2,256,128]{3,2,1,0:T(8,128)(2,1)S(1)} custom-call(s32[1]{0:T(128)} %bitcast.place_ref, s32[2,256]{1,0:T(2,128)S(1)} %copy-done.3, f32[8,2,256,128]{3,2,1,0:T(8,128)} %near.1.near_ref, bf16[1,2,256,128]{3,2,1,0:T(8,128)(2,1)} %copy-done.5, bf16[1,2,256,128]{3,2,1,0:T(8,128)(2,1)} %copy-done.4, bf16[8,3,2,256,256]{4,3,2,1,0:T(8,128)(2,1)} %blocks_hbm.1), custom_call_target="tpu_custom_call" | custom-call | tf_op jit(solution)/shard_map/rim/pallas_call | solution.py:367
  75.2 1.6 %unpack.1 = bf16[8,2,256,128]{3,2,1,0:T(8,128)(2,1)} custom-call(bf16[8,2,256,128]{3,2,1,0:T(8,128)(2,1)S(1)} %rim.1.near_ref, bf16[256,256]{1,0:T(8,128)(2,1)S(1)} %copy-done.2, bf16[32,4,16,256]{3,2,1,0:T(8,128)(2,1)S(1)} %all-to-all-done.1.refs_0_), custom_call_target="tpu_custom_call" | custom-call | tf_op jit(solution)/shard_map/unpack/pallas_call | solution.py:176
  (25 shorter events, 0.6 us)
Async XLA Ops:
  2.8 31.2 %all-to-all-start = ((bf16[32,4,16,256]{3,2,1,0:T(8,128)(2,1)}), bf16[32,4,16,256]{3,2,1,0:T(8,128)(2,1)S(1)}, u32[]{:S(2)}, u32[]{:S(2)}) async-start(bf16[32,4,16,256]{3,2,1,0:T(8,128)(2,1)} %pack.1), calls=%async_computation | async-start | bytes 2097152 | tf_op jit(solution)/shard_map/all_to_all | solution.py:402
  11.2 31.9 %copy-start.1 = (bf16[8,2,256,128]{3,2,1,0:T(8,128)(2,1)S(1)}, bf16[8,2,256,128]{3,2,1,0:T(8,128)(2,1)}, u32[]{:S(2)}) copy-start(bf16[8,2,256,128]{3,2,1,0:T(8,128)(2,1)} %currents_ref.3) | copy-start | bytes 3145732
  12.6 35.0 %copy-start.3 = (s32[2,256]{1,0:T(2,128)S(1)}, s32[2,256]{1,0:T(2,128)}, u32[]{:S(2)}) copy-start(s32[2,256]{1,0:T(2,128)} %mask_ref.3) | copy-start | bytes 6148
  38.2 37.0 %all-to-all-start.1 = ((bf16[32,4,16,256]{3,2,1,0:T(8,128)(2,1)}), bf16[32,4,16,256]{3,2,1,0:T(8,128)(2,1)S(1)}, u32[]{:S(2)}, u32[]{:S(2)}) async-start(bf16[32,4,16,256]{3,2,1,0:T(8,128)(2,1)} %far.1), calls=%async_computation.1 | async-start | bytes 2097152 | tf_op jit(solution)/shard_map/all_to_all | solution.py:402
  43.2 27.7 %collective-permute-start.1 = (bf16[1,2,256,128]{3,2,1,0:T(8,128)(2,1)S(1)}, bf16[1,2,256,128]{3,2,1,0:T(8,128)(2,1)S(1)}, u32[]{:S(2)}, u32[]{:S(2)}) collective-permute-start(bf16[1,2,256,128]{3,2,1,0:T(8,128)(2,1)S(1)} %get-tuple-element.5), channel_id=1, source_target_pairs={{1,2},{3,4},{5,6},{7,8},{9,10},{11,12},{13,14},{15,16},{17,18},{19... | collective-permute-start | bytes 393224 | tf_op jit(solution)/shard_map/ppermute | solution.py:389
  46.3 24.6 %collective-permute-start = (bf16[1,2,256,128]{3,2,1,0:T(8,128)(2,1)S(1)}, bf16[1,2,256,128]{3,2,1,0:T(8,128)(2,1)S(1)}, u32[]{:S(2)}, u32[]{:S(2)}) collective-permute-start(bf16[1,2,256,128]{3,2,1,0:T(8,128)(2,1)S(1)} %get-tuple-element.6), channel_id=1, source_target_pairs={{0,1},{1,0},{2,3},{3,2},{4,5},{5,4},{6,7},{7,6},{8,9},{9,8},{10,11... | collective-permute-start | bytes 393224 | tf_op jit(solution)/shard_map/ppermute | solution.py:388
  47.6 2.8 %copy-start = (bf16[8,3,2,256,256]{4,3,2,1,0:T(8,128)(2,1)S(1)}, bf16[8,3,2,256,256]{4,3,2,1,0:T(8,128)(2,1)}, u32[]{:S(2)}) copy-start(bf16[8,3,2,256,256]{4,3,2,1,0:T(8,128)(2,1)} %blocks_hbm.1) | copy-start | bytes 18874372
  55.7 19.5 %copy-start.2 = (bf16[256,256]{1,0:T(8,128)(2,1)S(1)}, bf16[256,256]{1,0:T(8,128)(2,1)}, u32[]{:S(2)}) copy-start(bf16[256,256]{1,0:T(8,128)(2,1)} %constant.40.clone.swap_ref) | copy-start | bytes 393220
  70.9 0.6 copy-start.4
  71.5 0.6 copy-start.5
